TPU v7x, 32 devices: a whole 2x2x4 slice. The times are simulated.
32 devices in a mesh: chan: 4 (over y, x), facet: 8 (over z, core).
Axes of the slice: x: 2, y: 2, z: 4, core: 2. Of those that a mesh axis runs over, the one named last changes fastest.
Arguments:
- image_field: float32 [4, 2048, 2048], P('chan', 'facet'), may hold values from -6 to 6
- weights: bfloat16 [4, 2048, 2048], P('chan', None, 'facet'), may hold values from 0.049804688 to 1
- measured: bfloat16 [4, 2, 2048, 2048], P('chan', None, None, 'facet'), may hold values from -6 to 6
- dual_field: bfloat16 [4, 2, 2048, 2048], P(None, None, 'facet', 'chan'), may hold values from -3 to 3
Outputs:
- image_next: float32 [4, 2048, 2048], P(None, 'facet', 'chan')
- dual_next: bfloat16 [4, 2, 2048, 2048], P(None, None, 'facet', 'chan')
All inputs are finite; a program needn't handle non-finite values.
Results may differ from a plain program's by a relative error of at most 0.001.
Values sent between devices are 32-bit elements; how exact they have to be, the bound alone decides.
A program may use at most 128 MiB of HBM per device.

v0:
```python
from functools import partial
import math

import jax
import jax.numpy as jnp
from jax import lax
from jax.sharding import PartitionSpec as P

FIRST = 64
SECOND = 32


step_primal = 0.5
step_dual = 0.5
clip_radius = 4.0


def passed_along(x, axis, by):
    devices = lax.axis_size(axis)
    pairs = [(i, i + by) for i in range(devices) if 0 <= i + by < devices]
    return lax.ppermute(x, axis, pairs)


def product(form, first_real, first_imag, table_real, table_imag):
    contract = partial(jnp.einsum, form, precision=lax.Precision.HIGHEST)
    if first_imag is None:
        return (contract(first_real, table_real), contract(first_real, table_imag))
    out_real = contract(first_real, table_real) - contract(first_imag, table_imag)
    out_imag = contract(first_real, table_imag) + contract(first_imag, table_real)
    return (out_real, out_imag)


def factor_tables(rotation):
    outer = jnp.arange(FIRST, dtype=jnp.int32)
    inner = jnp.arange(SECOND, dtype=jnp.int32)
    outer_phases = (
        2.0 * math.pi / FIRST * (outer[:, None] * outer[None, :] % FIRST).astype(jnp.float32)
    )
    inner_phases = (
        2.0 * math.pi / SECOND * (inner[:, None] * inner[None, :] % SECOND).astype(jnp.float32)
    )
    twiddle_phases = (
        2.0 * math.pi / (FIRST * SECOND) * (inner[:, None] * outer[None, :]).astype(jnp.float32)
    )
    return (
        jnp.cos(outer_phases),
        rotation * jnp.sin(outer_phases),
        jnp.cos(twiddle_phases),
        rotation * jnp.sin(twiddle_phases),
        jnp.cos(inner_phases),
        rotation * jnp.sin(inner_phases),
    )


def along_last(real_part, imag_part, rotation, real_only):
    leading = real_part.shape[:-1]
    new_shape = leading + (FIRST, SECOND)
    real_part = real_part.reshape(new_shape)
    if imag_part is not None:
        imag_part = imag_part.reshape(new_shape)
    table_real, table_imag, twiddle_real, twiddle_imag, inner_real, inner_imag = factor_tables(
        rotation
    )
    section_real, section_imag = product(
        "...ab,ka->...bk", real_part, imag_part, table_real, table_imag
    )
    turned_real = section_real * twiddle_real - section_imag * twiddle_imag
    turned_imag = section_real * twiddle_imag + section_imag * twiddle_real
    contract = partial(jnp.einsum, "...bk,bm->...mk", precision=lax.Precision.HIGHEST)
    if real_only:
        return (contract(turned_real, inner_real) - contract(turned_imag, inner_imag)).reshape(
            leading + (FIRST * SECOND,)
        )
    out_real, out_imag = product(
        "...bk,bm->...mk", turned_real, turned_imag, inner_real, inner_imag
    )
    return (
        out_real.reshape(leading + (FIRST * SECOND,)),
        out_imag.reshape(leading + (FIRST * SECOND,)),
    )


def along_first(real_part, imag_part, rotation):
    columns = real_part.shape[1]
    new_shape = (FIRST, SECOND, columns)
    table_real, table_imag, twiddle_real, twiddle_imag, inner_real, inner_imag = factor_tables(
        rotation
    )
    section_real, section_imag = product(
        "abc,ka->bkc",
        real_part.reshape(new_shape),
        imag_part.reshape(new_shape),
        table_real,
        table_imag,
    )
    turned_real = section_real * twiddle_real[:, :, None] - section_imag * twiddle_imag[:, :, None]
    turned_imag = section_real * twiddle_imag[:, :, None] + section_imag * twiddle_real[:, :, None]
    out_real, out_imag = product("bkc,bm->mkc", turned_real, turned_imag, inner_real, inner_imag)
    return (
        out_real.reshape((FIRST * SECOND, columns)),
        out_imag.reshape((FIRST * SECOND, columns)),
    )


def shards(image_field, weights, measured, dual_field):
    scale = 1.0 / (FIRST * SECOND)
    rows_real, rows_imag = along_last(image_field[0], None, -1.0, False)
    cols_real, cols_imag = (
        lax.all_to_all(rows_real, "facet", split_axis=1, concat_axis=0, tiled=True),
        lax.all_to_all(rows_imag, "facet", split_axis=1, concat_axis=0, tiled=True),
    )
    spec_real, spec_imag = along_first(cols_real, cols_imag, -1.0)
    weight_values = weights[0].astype(jnp.float32)
    resid_real = weight_values * (spec_real * scale) - measured[0, 0].astype(jnp.float32)
    resid_imag = weight_values * (spec_imag * scale) - measured[0, 1].astype(jnp.float32)
    back_real, back_imag = along_first(resid_real, resid_imag, 1.0)
    line_real, line_imag = (
        lax.all_to_all(back_real, "facet", split_axis=0, concat_axis=1, tiled=True),
        lax.all_to_all(back_imag, "facet", split_axis=0, concat_axis=1, tiled=True),
    )
    gradient = along_last(line_real, line_imag, 1.0, True) * scale
    image_tile, gradient_tile = (
        lax.all_to_all(image_field, "chan", split_axis=2, concat_axis=0, tiled=True),
        lax.all_to_all(gradient[None], "chan", split_axis=2, concat_axis=0, tiled=True),
    )
    dual_rows = dual_field[:, 0].astype(jnp.float32)
    dual_cols = dual_field[:, 1].astype(jnp.float32)
    above = passed_along(dual_rows[:, -1:, :], "facet", 1)
    leftward = passed_along(dual_cols[:, :, -1], "chan", 1)
    prev_rows = jnp.concatenate([above, dual_rows[:, :-1, :]], axis=1)
    prev_cols = jnp.concatenate([leftward[:, :, None], dual_cols[:, :, :-1]], axis=2)
    adjoint = prev_rows - dual_rows + prev_cols - dual_cols
    image_next = image_tile - step_primal * (gradient_tile + adjoint)
    extrapolated = 2.0 * image_next - image_tile
    below = passed_along(extrapolated[:, :1, :], "facet", -1)
    rightward = passed_along(extrapolated[:, :, 0], "chan", -1)
    diff_rows = jnp.concatenate([extrapolated[:, 1:, :], below], axis=1) - extrapolated
    diff_cols = (
        jnp.concatenate([extrapolated[:, :, 1:], rightward[:, :, None]], axis=2) - extrapolated
    )
    first_part = dual_rows + step_dual * diff_rows
    second_part = dual_cols + step_dual * diff_cols
    magnitude = jnp.sqrt(jnp.sum(first_part * first_part + second_part * second_part, axis=0))
    factor = 1.0 / jnp.maximum(1.0, magnitude / clip_radius)
    dual_next = jnp.stack([first_part * factor, second_part * factor], axis=1).astype(jnp.bfloat16)
    return (image_next, dual_next)


def solution(mesh):
    placed = (
        P("chan", "facet", None),
        P("chan", None, "facet"),
        P("chan", None, None, "facet"),
        P(None, None, "facet", "chan"),
    )
    return jax.shard_map(
        shards,
        mesh=mesh,
        in_specs=placed,
        out_specs=(P(None, "facet", "chan"), P(None, None, "facet", "chan")),
        check_vma=False,
    )
```

profile of v0, /device:TPU:7, one launch (start us, length us, event | category | flops | bytes accessed | tf_op | source)
XLA Modules:
  0.0 393.6 jit_solution(7630683436692505753)
XLA Ops:
  2.7 3.1 fusion.87
  5.8 5.5 %fusion.31 = (f32[256,32,64]{0,2,1:T(8,128)S(1)}, f32[256,32,64]{0,2,1:T(8,128)S(1)}) fusion(f32[64,256,32]{1,0,2:T(8,128)S(1)} %fusion.87, f32[32,64]{1,0:T(8,128)S(1)} %get-tuple-element.35, f32[32,64]{1,0:T(8,128)S(1)} %get-tuple-element.34, f32[256,64,32]{0,2,1:T(8,128)} %bitcast.201), kind=kOutput, calls=%fused_computation.55 | convolution fusion | flops 405860352 | bytes 8404992 | tf_op jit(solution)/shard_map/...ab,ka->...bk/dot_general | solution.py:27
  11.3 3.0 fusion.77
  14.4 3.0 add_bitcast_fusion
  20.0 5.8 %all-to-all-start.2 = ((f32[256,8,256]{0,2,1:T(8,128)}), f32[256,8,256]{0,2,1:T(8,128)}, u32[]{:S(2)}, u32[]{:S(2)}) async-start(f32[256,8,256]{0,2,1:T(8,128)} %bitcast.203), calls=%async_computation.2 | async-start | bytes 4194304 | tf_op jit(solution)/shard_map/all_to_all | solution.py:110
  25.8 4.6 %fusion.79 = f32[32,256,64]{1,0,2:T(8,128)S(1)} fusion(f32[256,32,64]{0,2,1:T(8,128)} %copy-done.6), kind=kOutput, calls=%fused_computation.113 | convolution fusion | flops 201341952 | bytes 4194304 | tf_op jit(solution)/shard_map/...bk,bm->...mk/dot_general | solution.py:28
  30.4 3.1 subtract_bitcast_fusion
  36.0 37.9 %all-to-all-done.2 = f32[256,8,256]{0,2,1:T(8,128)} async-done(((f32[256,8,256]{0,2,1:T(8,128)}), f32[256,8,256]{0,2,1:T(8,128)}, u32[]{:S(2)}, u32[]{:S(2)}) %all-to-all-start.2) | async-done | bytes 2097184 | tf_op jit(solution)/shard_map/all_to_all | solution.py:110
  73.9 5.6 %all-to-all-start.1 = ((f32[256,8,256]{0,2,1:T(8,128)}), f32[256,8,256]{0,2,1:T(8,128)}, u32[]{:S(2)}, u32[]{:S(2)}) async-start(f32[256,8,256]{0,2,1:T(8,128)} %bitcast.11), calls=%async_computation.1 | async-start | bytes 4194304 | tf_op jit(solution)/shard_map/all_to_all | solution.py:109
  82.7 4.4 %fusion.71 = f32[64,32,256]{2,0,1:T(8,128)} fusion(f32[64,32,256]{2,1,0:T(8,128)S(1)} %bitcast.196), kind=kOutput, calls=%fused_computation.105 | convolution fusion | flops 402714624 | bytes 4194304 | tf_op jit(solution)/shard_map/abc,ka->bkc/dot_general | solution.py:28
  87.2 4.4 %fusion.69 = f32[64,32,256]{2,0,1:T(8,128)} fusion(f32[64,32,256]{2,1,0:T(8,128)S(1)} %bitcast.197), kind=kOutput, calls=%fused_computation.103 | convolution fusion | flops 402710528 | bytes 4194304 | tf_op jit(solution)/shard_map/abc,ka->bkc/dot_general | solution.py:29
  91.6 36.1 %all-to-all-done.1 = f32[256,8,256]{0,2,1:T(8,128)} async-done(((f32[256,8,256]{0,2,1:T(8,128)}), f32[256,8,256]{0,2,1:T(8,128)}, u32[]{:S(2)}, u32[]{:S(2)}) %all-to-all-start.1) | async-done | bytes 2097184 | tf_op jit(solution)/shard_map/all_to_all | solution.py:109
  130.1 4.9 %fusion.93 = f32[64,32,256]{2,0,1:T(8,128)S(1)} fusion(f32[64,32,256]{2,0,1:T(8,128)} %fusion.71, f32[64,32,256]{2,1,0:T(8,128)S(1)} %bitcast.194), kind=kOutput, calls=%fused_computation.123 | convolution fusion | flops 403234816 | bytes 6291456 | tf_op jit(solution)/shard_map/abc,ka->bkc/dot_general | solution.py:28
  135.1 3.9 fusion.29
  139.0 3.0 fusion.61
  142.0 3.2 fusion.63
  145.3 3.2 add_multiply_fusion
  149.7 3.2 subtract_multiply_fusion
  155.5 3.4 fusion.55
  158.9 3.1 fusion.53
  162.0 3.1 fusion.103
  165.2 3.9 %fusion.27 = (f32[32,64,256]{2,1,0:T(8,128)S(1)}, f32[32,64,256]{2,1,0:T(8,128)S(1)}) fusion(f32[64,32,256]{2,0,1:T(8,128)S(1)} %fusion.103, f32[32,64]{1,0:T(8,128)S(1)} %fusion.166, f32[32,64]{1,0:T(8,128)S(1)} %get-tuple-element.34, f32[64,32,256]{2,0,1:T(8,128)S(1)} %fusion.53, f32[64,32,256]{2,1,0:T(8,128)S(1)} %get-tuple-element.32), kind=kOutput, calls=%fused_computation.43 | convolution fusion | flops 406380544 | bytes 10502144 | tf_op jit(solution)/shard_map/abc,ka->bkc/dot_general | solution.py:29
  169.1 3.4 fusion.45
  172.6 3.0 fusion.112
  178.2 5.4 %all-to-all-start.4 = ((f32[8,256,256]{2,1,0:T(8,128)}), f32[8,256,256]{2,1,0:T(8,128)}, u32[]{:S(2)}, u32[]{:S(2)}) async-start(f32[8,256,256]{2,1,0:T(8,128)} %bitcast.204), calls=%async_computation.4 | async-start | bytes 4194304 | tf_op jit(solution)/shard_map/all_to_all | solution.py:119
  183.6 4.6 %fusion.47 = f32[32,64,256]{2,0,1:T(8,128)S(1)} fusion(f32[32,64,256]{2,1,0:T(8,128)} %copy-done.5), kind=kOutput, calls=%fused_computation.81 | convolution fusion | flops 201340928 | bytes 4194304 | tf_op jit(solution)/shard_map/bkc,bm->mkc/dot_general | solution.py:28
  188.2 3.1 fusion.109
  193.8 38.0 %all-to-all-done.4 = f32[8,256,256]{2,1,0:T(8,128)} async-done(((f32[8,256,256]{2,1,0:T(8,128)}), f32[8,256,256]{2,1,0:T(8,128)}, u32[]{:S(2)}, u32[]{:S(2)}) %all-to-all-start.4) | async-done | bytes 2097184 | tf_op jit(solution)/shard_map/all_to_all | solution.py:119
  231.8 5.6 %all-to-all-start.3 = ((f32[8,256,256]{2,1,0:T(8,128)}), f32[8,256,256]{2,1,0:T(8,128)}, u32[]{:S(2)}, u32[]{:S(2)}) async-start(f32[8,256,256]{2,1,0:T(8,128)} %bitcast.202), calls=%async_computation.3 | async-start | bytes 4194304 | tf_op jit(solution)/shard_map/all_to_all | solution.py:118
  237.4 3.6 copy.94
  242.9 4.6 %fusion.39 = f32[256,32,64]{0,2,1:T(8,128)} fusion(f32[256,64,32]{0,2,1:T(8,128)S(1)} %bitcast.198), kind=kOutput, calls=%fused_computation.73 | convolution fusion | flops 402710528 | bytes 4194304 | tf_op jit(solution)/shard_map/...ab,ka->...bk/dot_general | solution.py:28
  247.5 4.7 %fusion.37 = f32[256,32,64]{0,2,1:T(8,128)} fusion(f32[256,64,32]{0,2,1:T(8,128)S(1)} %bitcast.199), kind=kOutput, calls=%fused_computation.71 | convolution fusion | flops 402710528 | bytes 4194304 | tf_op jit(solution)/shard_map/...ab,ka->...bk/dot_general | solution.py:29
  252.3 33.3 %all-to-all-done.3 = f32[8,256,256]{2,1,0:T(8,128)} async-done(((f32[8,256,256]{2,1,0:T(8,128)}), f32[8,256,256]{2,1,0:T(8,128)}, u32[]{:S(2)}, u32[]{:S(2)}) %all-to-all-start.3) | async-done | bytes 2097184 | tf_op jit(solution)/shard_map/all_to_all | solution.py:118
  285.5 4.6 %all-to-all-start = ((f32[1,256,2048]{1,0,2:T(1,128)}), f32[1,256,2048]{1,0,2:T(1,128)}, u32[]{:S(2)}, u32[]{:S(2)}) async-start(f32[1,256,2048]{1,0,2:T(1,128)} %copy.94), calls=%async_computation | async-start | bytes 4194304 | tf_op jit(solution)/shard_map/all_to_all | solution.py:123
  292.5 5.1 %fusion.115 = f32[256,32,64]{0,2,1:T(8,128)S(1)} fusion(f32[256,32,64]{0,2,1:T(8,128)} %fusion.39, f32[256,64,32]{0,2,1:T(8,128)S(1)} %bitcast.192), kind=kOutput, calls=%fused_computation.129 | convolution fusion | flops 403234816 | bytes 6291456 | tf_op jit(solution)/shard_map/...ab,ka->...bk/dot_general | solution.py:28
  297.6 4.4 %multiply_subtract_fusion.1 = (f32[256,32,64]{0,2,1:T(8,128)S(1)}, f32[256,32,64]{0,2,1:T(8,128)S(1)}) fusion(f32[256,32,64]{0,2,1:T(8,128)S(1)} %fusion.115, f32[32,64]{1,0:T(8,128)S(1)} %fusion.166, f32[32,64]{1,0:T(8,128)S(1)} %get-tuple-element.34, f32[256,32,64]{0,2,1:T(8,128)S(1)} %copy-done.12, f32[256,64,32]{0,2,1:T(8,128)S(1)} %bitcast.193), kind=kOutput, calls=%fused_computation.66 | convolution fusion | flops 406380544 | bytes 10502144 | tf_op jit(solution)/shard_map/...ab,ka->...bk/dot_general | solution.py:29
  305.0 3.4 multiply_bitcast_fusion
  309.6 10.0 %copy.135 = f32[1,256,2048]{1,0,2:T(1,128)} copy(f32[1,256,2048]{1,2,0:T(8,128)S(1)} %bitcast.205) | data formatting | bytes 4194304 | tf_op jit(solution)/shard_map/mul | solution.py:121
  319.5 4.5 %all-to-all-start.5 = ((f32[1,256,2048]{1,0,2:T(1,128)}), f32[1,256,2048]{1,0,2:T(1,128)}, u32[]{:S(2)}, u32[]{:S(2)}) async-start(f32[1,256,2048]{1,0,2:T(1,128)} %copy.135), calls=%async_computation.5 | async-start | bytes 4194304 | tf_op jit(solution)/shard_map/all_to_all | solution.py:124
  332.8 4.0 %slice_bitcast_fusion.2 = (f32[4,1,256,511]{2,3,0,1:T(8,128)}, f32[4,256,511]{1,2,0:T(8,128)}) fusion(f32[4,256,512]{1,2,0:T(8,128)} %copy-done.10), kind=kLoop, calls=%fused_computation.323 | loop fusion | bytes 6279168 | tf_op jit(solution)/shard_map/concatenate | solution.py:131
  339.1 7.9 %collective-permute-done.1 = f32[4,256]{1,0:T(4,128)S(1)} collective-permute-done((f32[4,256]{1,0:T(4,128)S(1)}, f32[4,256]{1,0:T(4,128)S(1)}, u32[]{:S(2)}, u32[]{:S(2)}) %collective-permute-start.1) | collective-permute-done | bytes 4128 | tf_op jit(solution)/shard_map/ppermute | solution.py:21
  349.7 3.0 copy.158
  355.6 4.7 %multiply_subtract_fusion = (f32[4,256,512]{1,2,0:T(8,128)S(1)}, f32[4,256,512]{1,2,0:T(8,128)}) fusion(f32[4,256,512]{1,2,0:T(8,128)S(1)} %bitcast.189, f32[4,256,512]{1,2,0:T(8,128)S(1)} %bitcast.190, bf16[4,1,256,512]{2,3,0,1:T(8,128)(2,1)S(1)} %copy.161, f32[4,256,511]{1,2,0:T(8,128)} %get-tuple-element.25, f32[4,256,1]{1,2,0:T(1,128)S(1)} %broadcast_in_dim.4, ...), kind=kLoop, calls=%fused_computation.63 | loop fusion | flops 6291456 | bytes 14680064 | tf_op jit(solution)/shard_map/sub | solution.py:134
  365.3 3.6 collective-permute-start.2
  368.9 3.1 collective-permute-start.3
  374.7 3.1 copy.152
  379.2 3.8 fusion.22
  384.6 5.7 %fusion.4 = (bf16[4,1,256,512]{2,3,0,1:T(8,128)(2,1)S(1)}, f32[4,1,256,512]{2,3,0,1:T(8,128)S(1)}) fusion(bf16[4,1,256,512]{2,3,0,1:T(8,128)(2,1)S(1)} %copy-done.2, f32[4,1,1,512]{2,3,0,1:T(8,128)} %copy.145, f32[4,1,255,512]{2,3,0,1:T(8,128)} %get-tuple-element.27, f32[256,512]{0,1:T(8,128)S(1)} %maximum_divide_fusion, f32[4,1,256,512]{2,3,0,1:T(8,128)} %bitcast.188, ...), kind=kLoop, calls=%fused_computation.12 | loop fusion | flops 9437184 | bytes 16252928 | tf_op jit(solution)/shard_map/convert.5
  (91 shorter events, 60.2 us)
Async XLA Ops:
  2.6 3.1 copy-start.7
  11.3 3.1 copy-start.6
  20.0 53.9 %all-to-all-start.2 = ((f32[256,8,256]{0,2,1:T(8,128)}), f32[256,8,256]{0,2,1:T(8,128)}, u32[]{:S(2)}, u32[]{:S(2)}) async-start(f32[256,8,256]{0,2,1:T(8,128)} %bitcast.203), calls=%async_computation.2 | async-start | bytes 4194304 | tf_op jit(solution)/shard_map/all_to_all | solution.py:110
  73.9 5.7 %copy-start.17 = (bf16[1,2,2048,256]{3,2,1,0:T(8,128)(2,1)S(1)}, bf16[1,2,2048,256]{3,2,1,0:T(8,128)(2,1)}, u32[]{:S(2)}) copy-start(bf16[1,2,2048,256]{3,2,1,0:T(8,128)(2,1)} %param.6) | copy-start | bytes 6291460
  73.9 53.8 %all-to-all-start.1 = ((f32[256,8,256]{0,2,1:T(8,128)}), f32[256,8,256]{0,2,1:T(8,128)}, u32[]{:S(2)}, u32[]{:S(2)}) async-start(f32[256,8,256]{0,2,1:T(8,128)} %bitcast.11), calls=%async_computation.1 | async-start | bytes 4194304 | tf_op jit(solution)/shard_map/all_to_all | solution.py:109
  130.1 4.9 %copy-start.13 = (f32[64,32,256]{2,0,1:T(8,128)S(1)}, f32[64,32,256]{2,0,1:T(8,128)}, u32[]{:S(2)}) copy-start(f32[64,32,256]{2,0,1:T(8,128)} %fusion.69) | copy-start | bytes 6291460
  152.9 1.2 copy-start.16
  152.9 1.5 copy-start.18
  169.1 3.5 copy-start.5
  178.2 53.6 %all-to-all-start.4 = ((f32[8,256,256]{2,1,0:T(8,128)}), f32[8,256,256]{2,1,0:T(8,128)}, u32[]{:S(2)}, u32[]{:S(2)}) async-start(f32[8,256,256]{2,1,0:T(8,128)} %bitcast.204), calls=%async_computation.4 | async-start | bytes 4194304 | tf_op jit(solution)/shard_map/all_to_all | solution.py:119
  231.8 5.6 %copy-start.14 = (f32[1,256,2048]{2,1,0:T(8,128)S(1)}, f32[1,256,2048]{2,1,0:T(8,128)}, u32[]{:S(2)}) copy-start(f32[1,256,2048]{2,1,0:T(8,128)} %param.4) | copy-start | bytes 6291460
  231.8 53.7 %all-to-all-start.3 = ((f32[8,256,256]{2,1,0:T(8,128)}), f32[8,256,256]{2,1,0:T(8,128)}, u32[]{:S(2)}, u32[]{:S(2)}) async-start(f32[8,256,256]{2,1,0:T(8,128)} %bitcast.202), calls=%async_computation.3 | async-start | bytes 4194304 | tf_op jit(solution)/shard_map/all_to_all | solution.py:118
  285.5 34.0 %all-to-all-start = ((f32[1,256,2048]{1,0,2:T(1,128)}), f32[1,256,2048]{1,0,2:T(1,128)}, u32[]{:S(2)}, u32[]{:S(2)}) async-start(f32[1,256,2048]{1,0,2:T(1,128)} %copy.94), calls=%async_computation | async-start | bytes 4194304 | tf_op jit(solution)/shard_map/all_to_all | solution.py:123
  292.4 5.1 %copy-start.12 = (f32[256,32,64]{0,2,1:T(8,128)S(1)}, f32[256,32,64]{0,2,1:T(8,128)}, u32[]{:S(2)}) copy-start(f32[256,32,64]{0,2,1:T(8,128)} %fusion.37) | copy-start | bytes 6291460
  319.5 33.2 %all-to-all-start.5 = ((f32[1,256,2048]{1,0,2:T(1,128)}), f32[1,256,2048]{1,0,2:T(1,128)}, u32[]{:S(2)}, u32[]{:S(2)}) async-start(f32[1,256,2048]{1,0,2:T(1,128)} %copy.135), calls=%async_computation.5 | async-start | bytes 4194304 | tf_op jit(solution)/shard_map/all_to_all | solution.py:124
  326.5 1.3 copy-start.10
  326.6 20.5 %collective-permute-start.1 = (f32[4,256]{1,0:T(4,128)S(1)}, f32[4,256]{1,0:T(4,128)S(1)}, u32[]{:S(2)}, u32[]{:S(2)}) collective-permute-start(f32[4,256]{1,0:T(4,128)S(1)} %bitcast.215), channel_id=1, source_target_pairs={{0,8},{8,16},{16,24},{1,9},{9,17},{17,25},{2,10},{10,18},{18,26},{... | collective-permute-start | bytes 12296 | tf_op jit(solution)/shard_map/ppermute | solution.py:21
  328.4 2.0 copy-start
  328.6 1.4 copy-start.8
  330.7 6.1 %copy-start.9 = (f32[4,256,512]{1,2,0:T(8,128)S(1)}, f32[4,256,512]{1,2,0:T(8,128)}, u32[]{:S(2)}) copy-start(f32[4,256,512]{1,2,0:T(8,128)} %copy-done.8) | copy-start | bytes 6291460
  330.7 16.3 %collective-permute-start = (f32[4,1,512]{2,0,1:T(4,128)S(1)}, f32[4,1,512]{2,0,1:T(4,128)S(1)}, u32[]{:S(2)}, u32[]{:S(2)}) collective-permute-start(f32[4,1,512]{2,0,1:T(4,128)S(1)} %copy.137), channel_id=1, source_target_pairs={{0,1},{1,2},{2,3},{3,4},{4,5},{5,6},{6,7},{8,9},{9,10},{10,11},{11... | collective-permute-start | bytes 24584 | tf_op jit(solution)/shard_map/ppermute | solution.py:21
  352.8 1.9 copy-start.1
  352.8 2.5 copy-start.3
  352.8 2.8 copy-start.15
  354.7 5.6 %copy-start.4 = (f32[1,256,2048]{1,2,0:T(8,128)}, f32[1,256,2048]{1,2,0:T(8,128)S(1)}, u32[]{:S(2)}) copy-start(f32[1,256,2048]{1,2,0:T(8,128)S(1)} %copy.159) | copy-start | bytes 6291460
  365.3 12.5 %collective-permute-start.2 = (f32[4,1,512]{2,0,1:T(4,128)S(1)}, f32[4,1,512]{2,0,1:T(4,128)S(1)}, u32[]{:S(2)}, u32[]{:S(2)}) collective-permute-start(f32[4,1,512]{2,0,1:T(4,128)S(1)} %copy.144), channel_id=1, source_target_pairs={{1,0},{2,1},{3,2},{4,3},{5,4},{6,5},{7,6},{9,8},{10,9},{11,10},{12... | collective-permute-start | bytes 24584 | tf_op jit(solution)/shard_map/ppermute | solution.py:21
  368.9 8.9 %collective-permute-start.3 = (f32[4,256]{1,0:T(4,128)S(1)}, f32[4,256]{1,0:T(4,128)S(1)}, u32[]{:S(2)}, u32[]{:S(2)}) collective-permute-start(f32[4,256]{1,0:T(4,128)S(1)} %bitcast.216), channel_id=1, source_target_pairs={{8,0},{16,8},{24,16},{9,1},{17,9},{25,17},{10,2},{18,10},{26,18},{... | collective-permute-start | bytes 12296 | tf_op jit(solution)/shard_map/ppermute | solution.py:21
  383.0 1.6 copy-start.2
  384.6 5.7 %copy-start.11 = (f32[4,1,256,511]{2,3,0,1:T(8,128)S(1)}, f32[4,1,256,511]{2,3,0,1:T(8,128)}, u32[]{:S(2)}) copy-start(f32[4,1,256,511]{2,3,0,1:T(8,128)} %get-tuple-element.20) | copy-start | bytes 6279172
where the time goes:
time: 399 us; the launch traced here: 394 us
  waiting for transfers between devices  153 us (38%)
  matrix products  105 us (26%)
  local copies, waits for them, and re-layouts  74.9 us (19%)
  starting transfers between devices  41.7 us (10%)
  other arithmetic  16.8 us (4%)
    all_to_all x1, waiting for transfers between devices, shards(): lax.all_to_all(back_imag, 'facet', split_axis=0, concat_axis=1, tiled=True)  38 us
    all_to_all x1, waiting for transfers between devices, shards(): lax.all_to_all(rows_imag, 'facet', split_axis=1, concat_axis=0, tiled=True)  37.9 us
    all_to_all x1, waiting for transfers between devices, shards(): lax.all_to_all(rows_real, 'facet', split_axis=1, concat_axis=0, tiled=True)  36.1 us
    all_to_all x1, waiting for transfers between devices, shards(): lax.all_to_all(back_real, 'facet', split_axis=0, concat_axis=1, tiled=True)  33.3 us
    dot_general x6, matrix products, product(): contract(first_imag, table_imag)  24.8 us
    dot_general x6, matrix products, product(): contract(first_real, table_real) - contract(first_imag, table_imag)  22.4 us
    dot_general x6, matrix products, product(): contract(first_imag, table_real)  21.8 us
    dot_general x6, matrix products, product(): contract(first_real, table_imag) + contract(first_imag, table_real)  21.5 us
  transfers between devices with their start and end apart: 10, of which 5 were waited for; matrix products, arithmetic and copies ran while one was open for 25% of the time, Pallas kernels for 0%

commit v1 on v0

v1 whole, which is shorter than its diff:
```python
from functools import partial
import math

import jax
import jax.numpy as jnp
import numpy as np
from jax import lax
from jax.experimental import pallas as pl
from jax.experimental.pallas import tpu as pltpu
from jax.sharding import PartitionSpec as P

step_primal = 0.5
step_dual = 0.5
clip_radius = 4.0
LANES = 128


def passed_along(x, axis, by):
    devices = lax.axis_size(axis)
    pairs = [(i, i + by) for i in range(devices) if 0 <= i + by < devices]
    return lax.ppermute(x, axis, pairs)


def turned(real, imag, num, den, sign):
    num = num % den
    if num == 0:
        return real, imag
    if 4 * num == den:
        return (-imag, real) if sign > 0 else (imag, -real)
    c = math.cos(2.0 * math.pi * num / den)
    s = sign * math.sin(2.0 * math.pi * num / den)
    if 8 * num == den:
        h = math.sqrt(0.5)
        if sign > 0:
            return (real - imag) * h, (real + imag) * h
        return (real + imag) * h, (imag - real) * h
    return real * c - imag * s, real * s + imag * c


def block_dft(values, sign):
    n = len(values)
    if n == 1:
        return values
    even = block_dft(values[0::2], sign)
    odd = block_dft(values[1::2], sign)
    low, high = [], []
    for k in range(n // 2):
        er, ei = even[k]
        tr, ti = turned(*odd[k], k, n, sign)
        low.append((er + tr, ei + ti))
        high.append((er - tr, ei - ti))
    return low + high


def halves(x):
    high = x.astype(jnp.bfloat16)
    return high, (x - high.astype(jnp.float32)).astype(jnp.bfloat16)


def exact_dot(first, second, dims):
    (fh, fl), (sh, sl) = first, second
    dot = partial(
        lax.dot_general, dimension_numbers=(dims, ((), ())), preferred_element_type=jnp.float32
    )
    return dot(fh, sh) + (dot(fh, sl) + dot(fl, sh))


def tables(blocks, inner):
    n = blocks * inner
    b = np.arange(blocks)[:, None, None]
    a = np.arange(inner)[None, :, None]
    i = np.arange(inner)[None, None, :]
    phase = 2.0 * np.pi / n * (((blocks * a + b) * i) % n)
    out = []
    for t in (np.cos(phase), np.sin(phase)):
        t = t.astype(np.float32)
        high = t.astype(jnp.bfloat16)
        low = (t - high.astype(np.float32)).astype(jnp.bfloat16)
        out += [high, low]
    return np.stack(out)


def kernel(
    F, CH, x_ref, t_ref, w_hbm, m_hbm, image_ref, grad_ref,
    xt, z, send, recv, wb, mb, wf, mf, u, sendy, recvy, gt, g,
    in_sem, fs, fr, bs, br, cs, cr, xs, xr, ls,
):
    R, N = x_ref.shape
    A = N // F
    C = A // LANES
    T = N // CH
    RC = R // LANES
    scale = 1.0 / N
    me = lax.axis_index("facet")
    mine = lax.axis_index("chan")
    order = sorted(range(1, F), key=lambda o: abs(o - F // 2))

    load_w = pltpu.make_async_copy(w_hbm.at[0], wb, in_sem.at[0])
    load_m = pltpu.make_async_copy(m_hbm.at[0], mb, in_sem.at[1])
    load_w.start()
    load_m.start()

    barrier = pltpu.get_barrier_semaphore()
    for o in range(1, F):
        pl.semaphore_signal(
            barrier, inc=1, device_id={"facet": lax.rem(me + o, F)},
            device_id_type=pl.DeviceIdType.MESH,
        )
    for o in range(1, CH):
        pl.semaphore_signal(
            barrier, inc=1, device_id={"chan": lax.rem(mine + o, CH)},
            device_id_type=pl.DeviceIdType.MESH,
        )
    pl.semaphore_wait(barrier, F - 1 + CH - 1)

    image_copies = []
    for o in range(1, CH):
        d = lax.rem(mine + o, CH)
        copy = pltpu.make_async_remote_copy(
            src_ref=x_ref.at[:, pl.ds(pl.multiple_of(d * T, LANES), T)],
            dst_ref=image_ref.at[mine],
            send_sem=xs.at[o], recv_sem=xr.at[o],
            device_id={"chan": d}, device_id_type=pl.DeviceIdType.MESH,
        )
        copy.start()
        image_copies.append(copy)
    own = pltpu.make_async_copy(
        x_ref.at[:, pl.ds(pl.multiple_of(mine * T, LANES), T)], image_ref.at[mine], ls.at[0]
    )
    own.start()
    image_copies.append(own)

    for i in range(RC):
        for j in range(N // LANES):
            xt[i, j * LANES:(j + 1) * LANES, :] = x_ref[
                i * LANES:(i + 1) * LANES, j * LANES:(j + 1) * LANES
            ].T

    @pl.loop(0, F)
    def _(b):
        lines = pl.ds(b, A, stride=F)
        part = halves(jnp.concatenate([xt[i, lines, :].T for i in range(RC)], axis=0))
        z[b, :, 0:A] = exact_dot(part, (t_ref[0, b], t_ref[1, b]), ((1,), (0,)))
        z[b, :, A:2 * A] = -exact_dot(part, (t_ref[2, b], t_ref[3, b]), ((1,), (0,)))

    copies = []
    for c in range(C):
        lo = c * LANES

        @pl.loop(0, R // 8)
        def _(t):
            rows = pl.ds(pl.multiple_of(t * 8, 8), 8)
            values = [
                (z[b, rows, lo:lo + LANES], z[b, rows, A + lo:A + lo + LANES]) for b in range(F)
            ]
            for j, (re, im) in enumerate(block_dft(values, -1.0)):
                send[c, j, rows, 0:LANES] = re
                send[c, j, rows, LANES:2 * LANES] = im

        group = []
        for o in order:
            d = lax.rem(me + o, F)
            copy = pltpu.make_async_remote_copy(
                src_ref=send.at[c, d], dst_ref=recv.at[c, me],
                send_sem=fs.at[c, o], recv_sem=fr.at[c, o],
                device_id={"facet": d}, device_id_type=pl.DeviceIdType.MESH,
            )
            copy.start()
            group.append(copy)
        copy = pltpu.make_async_copy(send.at[c, me], recv.at[c, me], fr.at[c, 0])
        copy.start()
        group.append(copy)
        copies.append(group)

    load_w.wait()
    load_m.wait()

    @pl.loop(0, N // 16)
    def _(t):
        rows = pl.ds(pl.multiple_of(t * 16, 16), 16)
        for c in range(C):
            lo = c * LANES
            wf[c, rows, :] = wb[rows, lo:lo + LANES].astype(jnp.float32) * scale
            mf[c, 0, rows, :] = mb[0, rows, lo:lo + LANES].astype(jnp.float32)
            mf[c, 1, rows, :] = mb[1, rows, lo:lo + LANES].astype(jnp.float32)

    for c in range(C):
        lo = c * LANES
        for copy in copies[c]:
            copy.wait()

        @pl.loop(0, R // 8)
        def _(t):
            rows = pl.ds(pl.multiple_of(t * 8, 8), 8)
            values = [
                (recv[c, q, rows, 0:LANES], recv[c, q, rows, LANES:2 * LANES]) for q in range(F)
            ]
            for k, (re, im) in enumerate(block_dft(values, -1.0)):
                u[k, rows, 0:LANES] = re
                u[k, rows, LANES:2 * LANES] = im

        @pl.loop(0, F)
        def _(k):
            cos, sin = (t_ref[0, k], t_ref[1, k]), (t_ref[2, k], t_ref[3, k])
            part = halves(u[k])
            p = exact_dot(cos, part, ((1,), (0,)))
            q = exact_dot(sin, part, ((1,), (0,)))
            spec_re = p[:, 0:LANES] + q[:, LANES:]
            spec_im = p[:, LANES:] - q[:, 0:LANES]
            lines = pl.ds(k, A, stride=F)
            weight = wf[c, lines, :]
            res_re = weight * spec_re - mf[c, 0, lines, :]
            res_im = weight * spec_im - mf[c, 1, lines, :]
            part = halves(jnp.concatenate([res_re, res_im], axis=1))
            p = exact_dot(cos, part, ((0,), (0,)))
            q = exact_dot(sin, part, ((0,), (0,)))
            u[k, :, 0:LANES] = p[:, 0:LANES] - q[:, LANES:]
            u[k, :, LANES:2 * LANES] = p[:, LANES:] + q[:, 0:LANES]

        @pl.loop(0, R // 8)
        def _(t):
            rows = pl.ds(pl.multiple_of(t * 8, 8), 8)
            values = [(u[k, rows, 0:LANES], u[k, rows, LANES:2 * LANES]) for k in range(F)]
            for q, (re, im) in enumerate(block_dft(values, 1.0)):
                sendy[q, rows, lo:lo + LANES] = re
                sendy[q, rows, A + lo:A + lo + LANES] = im

    back = []
    for h in range(RC):
        rows = pl.ds(h * LANES, LANES)
        group = []
        for o in order:
            d = lax.rem(me + o, F)
            copy = pltpu.make_async_remote_copy(
                src_ref=sendy.at[d, rows], dst_ref=recvy.at[me, rows],
                send_sem=bs.at[h, o], recv_sem=br.at[h, o],
                device_id={"facet": d}, device_id_type=pl.DeviceIdType.MESH,
            )
            copy.start()
            group.append(copy)
        copy = pltpu.make_async_copy(sendy.at[me, rows], recvy.at[me, rows], br.at[h, 0])
        copy.start()
        group.append(copy)
        back.append(group)

    last = []
    for h in range(RC):
        for copy in back[h]:
            copy.wait()

        @pl.loop(0, LANES // 8)
        def _(t):
            rows = pl.ds(pl.multiple_of(h * LANES + t * 8, 8), 8)
            for c in range(C):
                lo = c * LANES
                values = [
                    (recvy[j, rows, lo:lo + LANES], recvy[j, rows, A + lo:A + lo + LANES])
                    for j in range(F)
                ]
                for b, (re, im) in enumerate(block_dft(values, 1.0)):
                    z[b, rows, lo:lo + LANES] = re
                    z[b, rows, A + lo:A + lo + LANES] = im

        span = pl.ds(h * LANES, LANES)

        @pl.loop(0, F)
        def _(b):
            re, im = halves(z[b, span, 0:A]), halves(z[b, span, A:2 * A])
            line = exact_dot((t_ref[0, b], t_ref[1, b]), re, ((1,), (1,))) - exact_dot(
                (t_ref[2, b], t_ref[3, b]), im, ((1,), (1,))
            )
            gt[pl.ds(b, A, stride=F), :] = line * scale

        for j in range(N // LANES):
            g[span, j * LANES:(j + 1) * LANES] = gt[j * LANES:(j + 1) * LANES, :].T
        for o in range(1, CH):
            d = lax.rem(mine + o, CH)
            copy = pltpu.make_async_remote_copy(
                src_ref=g.at[span, pl.ds(pl.multiple_of(d * T, LANES), T)],
                dst_ref=grad_ref.at[mine, span],
                send_sem=cs.at[h, o], recv_sem=cr.at[h, o],
                device_id={"chan": d}, device_id_type=pl.DeviceIdType.MESH,
            )
            copy.start()
            last.append(copy)
        copy = pltpu.make_async_copy(
            g.at[span, pl.ds(pl.multiple_of(mine * T, LANES), T)],
            grad_ref.at[mine, span], ls.at[1 + h],
        )
        copy.start()
        last.append(copy)
    for copy in image_copies + last:
        copy.wait()


def gradient_tiles(F, CH, image, weights, measured):
    R, N = image.shape
    A = N // F
    C = A // LANES
    RC = R // LANES
    table = jnp.asarray(tables(F, A))
    tile = jax.ShapeDtypeStruct((CH, R, N // CH), jnp.float32)
    f32 = jnp.float32
    dma = pltpu.SemaphoreType.DMA
    vmem = pl.BlockSpec(memory_space=pltpu.VMEM)
    hbm = pl.BlockSpec(memory_space=pl.ANY)
    return pl.pallas_call(
        partial(kernel, F, CH),
        out_shape=(tile, tile),
        in_specs=[vmem, vmem, hbm, hbm],
        out_specs=(vmem, vmem),
        scratch_shapes=[
            pltpu.VMEM((RC, N, LANES), f32),
            pltpu.VMEM((F, R, 2 * A), f32),
            pltpu.VMEM((C, F, R, 2 * LANES), f32),
            pltpu.VMEM((C, F, R, 2 * LANES), f32),
            pltpu.VMEM((N, A), jnp.bfloat16),
            pltpu.VMEM((2, N, A), jnp.bfloat16),
            pltpu.VMEM((C, N, LANES), f32),
            pltpu.VMEM((C, 2, N, LANES), f32),
            pltpu.VMEM((F, A, 2 * LANES), f32),
            pltpu.VMEM((F, R, 2 * A), f32),
            pltpu.VMEM((F, R, 2 * A), f32),
            pltpu.VMEM((N, LANES), f32),
            pltpu.VMEM((R, N), f32),
            dma((2,)),
            dma((C, F)), dma((C, F)),
            dma((RC, F)), dma((RC, F)),
            dma((RC, CH)), dma((RC, CH)),
            dma((CH,)), dma((CH,)),
            dma((1 + RC,)),
        ],
        compiler_params=pltpu.CompilerParams(
            collective_id=0, has_side_effects=True, vmem_limit_bytes=60 * 1024 * 1024
        ),
    )(image, table, weights, measured)


def shards(image_field, weights, measured, dual_field):
    image_tile, gradient_tile = gradient_tiles(
        lax.axis_size("facet"), lax.axis_size("chan"), image_field[0], weights, measured
    )
    dual_rows = dual_field[:, 0].astype(jnp.float32)
    dual_cols = dual_field[:, 1].astype(jnp.float32)
    above = passed_along(dual_rows[:, -1:, :], "facet", 1)
    leftward = passed_along(dual_cols[:, :, -1], "chan", 1)
    prev_rows = jnp.concatenate([above, dual_rows[:, :-1, :]], axis=1)
    prev_cols = jnp.concatenate([leftward[:, :, None], dual_cols[:, :, :-1]], axis=2)
    adjoint = prev_rows - dual_rows + prev_cols - dual_cols
    image_next = image_tile - step_primal * (gradient_tile + adjoint)
    extrapolated = 2.0 * image_next - image_tile
    below = passed_along(extrapolated[:, :1, :], "facet", -1)
    rightward = passed_along(extrapolated[:, :, 0], "chan", -1)
    diff_rows = jnp.concatenate([extrapolated[:, 1:, :], below], axis=1) - extrapolated
    diff_cols = (
        jnp.concatenate([extrapolated[:, :, 1:], rightward[:, :, None]], axis=2) - extrapolated
    )
    first_part = dual_rows + step_dual * diff_rows
    second_part = dual_cols + step_dual * diff_cols
    magnitude = jnp.sqrt(jnp.sum(first_part * first_part + second_part * second_part, axis=0))
    factor = 1.0 / jnp.maximum(1.0, magnitude / clip_radius)
    dual_next = jnp.stack([first_part * factor, second_part * factor], axis=1).astype(jnp.bfloat16)
    return (image_next, dual_next)


def solution(mesh):
    placed = (
        P("chan", "facet", None),
        P("chan", None, "facet"),
        P("chan", None, None, "facet"),
        P(None, None, "facet", "chan"),
    )
    return jax.shard_map(
        shards,
        mesh=mesh,
        in_specs=placed,
        out_specs=(P(None, "facet", "chan"), P(None, None, "facet", "chan")),
        check_vma=False,
    )
```

time: 399 us -> 250 us (0.63)
  the two profiles are of different devices: /device:TPU:7 before, /device:TPU:9 now
where the time goes in v1:
time: 250 us; the launch traced here: 245 us
  Pallas kernels  212 us (85%)
  other arithmetic  14 us (6%)
  starting transfers between devices  10.1 us (4%)
  local copies, waits for them, and re-layouts  7.8 us (3%)
    pallas_call x1, Pallas kernels, gradient_tiles(): pl.pallas_call(partial(kernel, F, CH), out_shape=(tile, tile), in_specs=[...  212 us
    ppermute x4, starting transfers between devices, passed_along(): return lax.ppermute(x, axis, pairs)  10.1 us
    sub x1, other arithmetic, shards(): extrapolated = 2.0 * image_next - image_tile  6.55 us
  transfers between devices with their start and end apart: 4, of which 1 were waited for; matrix products, arithmetic and copies ran while one was open for 2% of the time, Pallas kernels for 86%

profile of v1, /device:TPU:9, one launch (start us, length us, event | category | flops | bytes accessed | tf_op | source)
XLA Modules:
  0.0 245.2 jit_solution(10256822134961141107)
XLA Ops:
  0.6 1.9 bitcast_convert_fusion.1
  2.5 0.0 copy-start.4
  2.5 0.0 copy-start.3
  2.5 1.3 copy-done.4
  3.8 3.8 %collective-permute-start = (f32[4,1,512]{2,1,0:T(1,128)S(1)}, f32[4,1,512]{2,1,0:T(1,128)S(1)}, u32[]{:S(2)}, u32[]{:S(2)}) collective-permute-start(f32[4,1,512]{2,1,0:T(1,128)S(1)} %slice.40), channel_id=1, source_target_pairs={{0,1},{1,2},{2,3},{3,4},{4,5},{5,6},{6,7},{8,9},{9,10},{10,11},{11... | collective-permute-start | bytes 24584 | tf_op jit(solution)/shard_map/ppermute | solution.py:21
  7.6 0.4 slice_reduce_fusion.1
  8.0 3.1 %collective-permute-start.1 = (f32[4,256]{1,0:T(4,128)S(1)}, f32[4,256]{1,0:T(4,128)S(1)}, u32[]{:S(2)}, u32[]{:S(2)}) collective-permute-start(f32[4,256]{1,0:T(4,128)S(1)} %slice_reduce_fusion.1), channel_id=1, source_target_pairs={{0,8},{8,16},{16,24},{1,9},{9,17},{17,25},{2,10},{10,18},{18,26},{... | collective-permute-start | bytes 12296 | tf_op jit(solution)/shard_map/ppermute | solution.py:21
  11.1 211.9 %shard_map.68 = (f32[4,256,512]{2,1,0:T(8,128)}, f32[4,256,512]{2,1,0:T(8,128)}) custom-call(f32[256,2048]{1,0:T(8,128)} %bitcast.39, bf16[4,8,256,256]{3,2,1,0:T(8,128)(2,1)} %constant.13.clone.t_ref, bf16[1,2048,256]{2,1,0:T(8,128)(2,1)} %w_hbm.1, bf16[1,2,2048,256]{3,2,1,0:T(8,128)(2,1)} %m_hbm.1), custom_call_target="tpu_custom_call" | custom-call | tf_op jit(solution)/shard_map/pallas_call | solution.py:307
  223.0 0.0 copy-done.3
  223.0 0.0 collective-permute-done.1
  223.1 0.2 copy.19
  223.3 0.0 collective-permute-done
  223.3 6.5 %multiply_subtract_fusion = (f32[4,256,512]{2,1,0:T(8,128)S(1)}, f32[4,256,512]{2,1,0:T(8,128)}) fusion(f32[4,256,512]{2,1,0:T(8,128)} %get-tuple-element.4, f32[4,256,512]{2,1,0:T(8,128)} %get-tuple-element.5, bf16[4,2,256,512]{3,2,1,0:T(8,128)(2,1)} %param.8, f32[4,256,511]{2,1,0:T(8,128)} %bitcast.37, f32[4,256,1]{2,1,0:T(8,128)S(1)} %copy.19, ...), kind=kLoop, calls=%fused_computation.16 | loop fusion | flops 6291456 | bytes 14680064 | tf_op jit(solution)/shard_map/sub | solution.py:351
  229.8 1.9 collective-permute-start.2
  231.8 0.2 slice_reduce_fusion
  232.0 1.3 collective-permute-start.3
  233.3 1.9 slice.46
  235.2 1.6 slice.44
  236.8 0.0 collective-permute-done.3
  236.8 0.2 copy.20
  237.1 0.6 collective-permute-done.2
  237.7 0.0 copy-start
  237.7 0.0 copy-start.1
  237.7 0.0 copy-start.2
  237.7 4.2 %add_reduce_fusion = f32[256,512]{1,0:T(8,128)S(1)} fusion(f32[4,256,512]{2,1,0:T(8,128)S(1)} %get-tuple-element.12, f32[4,1,512]{2,1,0:T(1,128)S(1)} %collective-permute-done.2, f32[4,255,512]{2,1,0:T(8,128)} %slice.44, bf16[4,2,256,512]{3,2,1,0:T(8,128)(2,1)} %param.8, f32[4,256,1]{2,1,0:T(8,128)S(1)} %copy.20, f32[4,256,511]{2,1,0:T(8,128)} %slice.46), kind=kLoop, calls=%fused_computation.15 | loop fusion | flops 7208960 | bytes 8912896 | tf_op jit(solution)/shard_map/reduce_sum | solution.py:360
  241.8 0.2 maximum_divide_fusion
  242.0 0.0 copy-done
  242.1 0.0 copy-done.1
  242.1 0.3 copy-done.2
  242.4 1.1 fusion.9
  243.5 0.2 pad_maximum_fusion
  243.7 1.5 copy.21
  (2 shorter events, 0.0 us)
Async XLA Ops:
  2.5 1.3 copy-start.4
  2.5 220.5 %copy-start.3 = (f32[4,256,512]{2,1,0:T(8,128)}, f32[4,256,512]{2,1,0:T(8,128)S(1)}, u32[]{:S(2)}) copy-start(f32[4,256,512]{2,1,0:T(8,128)S(1)} %get-tuple-element.17) | copy-start | bytes 6291460
  3.8 219.4 %collective-permute-start = (f32[4,1,512]{2,1,0:T(1,128)S(1)}, f32[4,1,512]{2,1,0:T(1,128)S(1)}, u32[]{:S(2)}, u32[]{:S(2)}) collective-permute-start(f32[4,1,512]{2,1,0:T(1,128)S(1)} %slice.40), channel_id=1, source_target_pairs={{0,1},{1,2},{2,3},{3,4},{4,5},{5,6},{6,7},{8,9},{9,10},{10,11},{11... | collective-permute-start | bytes 24584 | tf_op jit(solution)/shard_map/ppermute | solution.py:21
  8.0 215.1 %collective-permute-start.1 = (f32[4,256]{1,0:T(4,128)S(1)}, f32[4,256]{1,0:T(4,128)S(1)}, u32[]{:S(2)}, u32[]{:S(2)}) collective-permute-start(f32[4,256]{1,0:T(4,128)S(1)} %slice_reduce_fusion.1), channel_id=1, source_target_pairs={{0,8},{8,16},{16,24},{1,9},{9,17},{17,25},{2,10},{10,18},{18,26},{... | collective-permute-start | bytes 12296 | tf_op jit(solution)/shard_map/ppermute | solution.py:21
  229.8 7.8 %collective-permute-start.2 = (f32[4,1,512]{2,1,0:T(1,128)S(1)}, f32[4,1,512]{2,1,0:T(1,128)S(1)}, u32[]{:S(2)}, u32[]{:S(2)}) collective-permute-start(f32[4,1,512]{2,1,0:T(1,128)S(1)} %slice.45), channel_id=1, source_target_pairs={{1,0},{2,1},{3,2},{4,3},{5,4},{6,5},{7,6},{9,8},{10,9},{11,10},{12... | collective-permute-start | bytes 24584 | tf_op jit(solution)/shard_map/ppermute | solution.py:21
  232.0 4.8 %collective-permute-start.3 = (f32[4,256]{1,0:T(4,128)S(1)}, f32[4,256]{1,0:T(4,128)S(1)}, u32[]{:S(2)}, u32[]{:S(2)}) collective-permute-start(f32[4,256]{1,0:T(4,128)S(1)} %slice_reduce_fusion), channel_id=1, source_target_pairs={{8,0},{16,8},{24,16},{9,1},{17,9},{25,17},{10,2},{18,10},{26,18},{... | collective-permute-start | bytes 12296 | tf_op jit(solution)/shard_map/ppermute | solution.py:21
  237.7 4.4 %copy-start = (bf16[4,2,256,512]{3,2,1,0:T(8,128)(2,1)S(1)}, bf16[4,2,256,512]{3,2,1,0:T(8,128)(2,1)}, u32[]{:S(2)}) copy-start(bf16[4,2,256,512]{3,2,1,0:T(8,128)(2,1)} %param.8) | copy-start | bytes 6291460
  237.7 4.4 %copy-start.1 = (f32[4,256,511]{2,1,0:T(8,128)S(1)}, f32[4,256,511]{2,1,0:T(8,128)}, u32[]{:S(2)}) copy-start(f32[4,256,511]{2,1,0:T(8,128)} %slice.46) | copy-start | bytes 6279172
  237.7 4.7 %copy-start.2 = (f32[4,255,512]{2,1,0:T(8,128)S(1)}, f32[4,255,512]{2,1,0:T(8,128)}, u32[]{:S(2)}) copy-start(f32[4,255,512]{2,1,0:T(8,128)} %slice.44) | copy-start | bytes 6266884

commit v2 on v1

--- a/solution.py
+++ b/solution.py
@@ -71,13 +71,23 @@
     a = np.arange(inner)[None, :, None]
     i = np.arange(inner)[None, None, :]
     phase = 2.0 * np.pi / n * (((blocks * a + b) * i) % n)
-    out = []
-    for t in (np.cos(phase), np.sin(phase)):
-        t = t.astype(np.float32)
-        high = t.astype(jnp.bfloat16)
-        low = (t - high.astype(np.float32)).astype(jnp.bfloat16)
-        out += [high, low]
-    return np.stack(out)
+    pair = np.stack([np.cos(phase), -np.sin(phase)], axis=2).astype(np.float32)
+    pair = pair.reshape(blocks, inner, 2, inner // LANES, LANES)
+    pair = pair.transpose(0, 1, 3, 2, 4).reshape(blocks, inner, 2 * inner)
+    high = pair.astype(jnp.bfloat16)
+    low = (pair - high.astype(np.float32)).astype(jnp.bfloat16)
+    return np.stack([high, low])
+
+
+def square_tables(t_ref, k, chunks):
+    found = []
+    for at in (0, LANES):
+        pieces = [
+            [t_ref[s, k, :, 2 * LANES * c + at:2 * LANES * c + at + LANES] for c in range(chunks)]
+            for s in (0, 1)
+        ]
+        found.append(tuple(jnp.concatenate(p, axis=1) if chunks > 1 else p[0] for p in pieces))
+    return found
 
 
 def kernel(
@@ -90,6 +100,7 @@
     C = A // LANES
     T = N // CH
     RC = R // LANES
+    W = 2 * LANES
     scale = 1.0 / N
     me = lax.axis_index("facet")
     mine = lax.axis_index("chan")
@@ -130,46 +141,47 @@
     own.start()
     image_copies.append(own)
 
-    for i in range(RC):
-        for j in range(N // LANES):
-            xt[i, j * LANES:(j + 1) * LANES, :] = x_ref[
-                i * LANES:(i + 1) * LANES, j * LANES:(j + 1) * LANES
-            ].T
-
-    @pl.loop(0, F)
-    def _(b):
-        lines = pl.ds(b, A, stride=F)
-        part = halves(jnp.concatenate([xt[i, lines, :].T for i in range(RC)], axis=0))
-        z[b, :, 0:A] = exact_dot(part, (t_ref[0, b], t_ref[1, b]), ((1,), (0,)))
-        z[b, :, A:2 * A] = -exact_dot(part, (t_ref[2, b], t_ref[3, b]), ((1,), (0,)))
-
     copies = []
     for c in range(C):
-        lo = c * LANES
-
-        @pl.loop(0, R // 8)
-        def _(t):
-            rows = pl.ds(pl.multiple_of(t * 8, 8), 8)
-            values = [
-                (z[b, rows, lo:lo + LANES], z[b, rows, A + lo:A + lo + LANES]) for b in range(F)
-            ]
-            for j, (re, im) in enumerate(block_dft(values, -1.0)):
-                send[c, j, rows, 0:LANES] = re
-                send[c, j, rows, LANES:2 * LANES] = im
-
+        wide = slice(c * W, (c + 1) * W)
         group = []
-        for o in order:
-            d = lax.rem(me + o, F)
-            copy = pltpu.make_async_remote_copy(
-                src_ref=send.at[c, d], dst_ref=recv.at[c, me],
-                send_sem=fs.at[c, o], recv_sem=fr.at[c, o],
-                device_id={"facet": d}, device_id_type=pl.DeviceIdType.MESH,
+        for h in range(RC):
+            if c == 0:
+                for j in range(N // LANES):
+                    xt[h, j * LANES:(j + 1) * LANES, :] = x_ref[
+                        h * LANES:(h + 1) * LANES, j * LANES:(j + 1) * LANES
+                    ].T
+
+            @pl.loop(0, F)
+            def _(b):
+                part = halves(xt[h, pl.ds(b, A, stride=F), :].T)
+                table = (t_ref[0, b, :, wide], t_ref[1, b, :, wide])
+                z[b, 0:LANES, 0:W] = exact_dot(part, table, ((1,), (0,)))
+
+            @pl.loop(0, LANES // 8)
+            def _(t):
+                rows = pl.ds(pl.multiple_of(t * 8, 8), 8)
+                target = pl.ds(pl.multiple_of(h * LANES + t * 8, 8), 8)
+                values = [(z[b, rows, 0:LANES], z[b, rows, LANES:W]) for b in range(F)]
+                for j, (re, im) in enumerate(block_dft(values, -1.0)):
+                    send[c, j, target, 0:LANES] = re
+                    send[c, j, target, LANES:W] = im
+
+            span = pl.ds(h * LANES, LANES)
+            for o in order:
+                d = lax.rem(me + o, F)
+                copy = pltpu.make_async_remote_copy(
+                    src_ref=send.at[c, d, span], dst_ref=recv.at[c, me, span],
+                    send_sem=fs.at[c, h, o], recv_sem=fr.at[c, h, o],
+                    device_id={"facet": d}, device_id_type=pl.DeviceIdType.MESH,
+                )
+                copy.start()
+                group.append(copy)
+            copy = pltpu.make_async_copy(
+                send.at[c, me, span], recv.at[c, me, span], fr.at[c, h, 0]
             )
             copy.start()
             group.append(copy)
-        copy = pltpu.make_async_copy(send.at[c, me], recv.at[c, me], fr.at[c, 0])
-        copy.start()
-        group.append(copy)
         copies.append(group)
 
     load_w.wait()
@@ -184,29 +196,28 @@
             mf[c, 0, rows, :] = mb[0, rows, lo:lo + LANES].astype(jnp.float32)
             mf[c, 1, rows, :] = mb[1, rows, lo:lo + LANES].astype(jnp.float32)
 
+    back = [[] for _ in range(RC)]
     for c in range(C):
-        lo = c * LANES
+        wide = slice(c * W, (c + 1) * W)
         for copy in copies[c]:
             copy.wait()
 
         @pl.loop(0, R // 8)
         def _(t):
             rows = pl.ds(pl.multiple_of(t * 8, 8), 8)
-            values = [
-                (recv[c, q, rows, 0:LANES], recv[c, q, rows, LANES:2 * LANES]) for q in range(F)
-            ]
+            values = [(recv[c, q, rows, 0:LANES], recv[c, q, rows, LANES:W]) for q in range(F)]
             for k, (re, im) in enumerate(block_dft(values, -1.0)):
                 u[k, rows, 0:LANES] = re
-                u[k, rows, LANES:2 * LANES] = im
+                u[k, rows, LANES:W] = im
 
         @pl.loop(0, F)
         def _(k):
-            cos, sin = (t_ref[0, k], t_ref[1, k]), (t_ref[2, k], t_ref[3, k])
+            cos, sin = square_tables(t_ref, k, C)
             part = halves(u[k])
             p = exact_dot(cos, part, ((1,), (0,)))
             q = exact_dot(sin, part, ((1,), (0,)))
-            spec_re = p[:, 0:LANES] + q[:, LANES:]
-            spec_im = p[:, LANES:] - q[:, 0:LANES]
+            spec_re = p[:, 0:LANES] - q[:, LANES:]
+            spec_im = p[:, LANES:] + q[:, 0:LANES]
             lines = pl.ds(k, A, stride=F)
             weight = wf[c, lines, :]
             res_re = weight * spec_re - mf[c, 0, lines, :]
@@ -214,34 +225,34 @@
             part = halves(jnp.concatenate([res_re, res_im], axis=1))
             p = exact_dot(cos, part, ((0,), (0,)))
             q = exact_dot(sin, part, ((0,), (0,)))
-            u[k, :, 0:LANES] = p[:, 0:LANES] - q[:, LANES:]
-            u[k, :, LANES:2 * LANES] = p[:, LANES:] + q[:, 0:LANES]
-
-        @pl.loop(0, R // 8)
-        def _(t):
-            rows = pl.ds(pl.multiple_of(t * 8, 8), 8)
-            values = [(u[k, rows, 0:LANES], u[k, rows, LANES:2 * LANES]) for k in range(F)]
-            for q, (re, im) in enumerate(block_dft(values, 1.0)):
-                sendy[q, rows, lo:lo + LANES] = re
-                sendy[q, rows, A + lo:A + lo + LANES] = im
-
-    back = []
-    for h in range(RC):
-        rows = pl.ds(h * LANES, LANES)
-        group = []
-        for o in order:
-            d = lax.rem(me + o, F)
-            copy = pltpu.make_async_remote_copy(
-                src_ref=sendy.at[d, rows], dst_ref=recvy.at[me, rows],
-                send_sem=bs.at[h, o], recv_sem=br.at[h, o],
-                device_id={"facet": d}, device_id_type=pl.DeviceIdType.MESH,
+            u[k, :, 0:LANES] = p[:, 0:LANES] + q[:, LANES:]
+            u[k, :, LANES:W] = p[:, LANES:] - q[:, 0:LANES]
+
+        for h in range(RC):
+
+            @pl.loop(0, LANES // 8)
+            def _(t):
+                rows = pl.ds(pl.multiple_of(h * LANES + t * 8, 8), 8)
+                values = [(u[k, rows, 0:LANES], u[k, rows, LANES:W]) for k in range(F)]
+                for q, (re, im) in enumerate(block_dft(values, 1.0)):
+                    sendy[q, rows, c * W:c * W + LANES] = re
+                    sendy[q, rows, c * W + LANES:(c + 1) * W] = im
+
+            span = pl.ds(h * LANES, LANES)
+            for o in order:
+                d = lax.rem(me + o, F)
+                copy = pltpu.make_async_remote_copy(
+                    src_ref=sendy.at[d, span, wide], dst_ref=recvy.at[me, span, wide],
+                    send_sem=bs.at[c, h, o], recv_sem=br.at[c, h, o],
+                    device_id={"facet": d}, device_id_type=pl.DeviceIdType.MESH,
+                )
+                copy.start()
+                back[h].append(copy)
+            copy = pltpu.make_async_copy(
+                sendy.at[me, span, wide], recvy.at[me, span, wide], br.at[c, h, 0]
             )
             copy.start()
-            group.append(copy)
-        copy = pltpu.make_async_copy(sendy.at[me, rows], recvy.at[me, rows], br.at[h, 0])
-        copy.start()
-        group.append(copy)
-        back.append(group)
+            back[h].append(copy)
 
     last = []
     for h in range(RC):
@@ -251,24 +262,19 @@
         @pl.loop(0, LANES // 8)
         def _(t):
             rows = pl.ds(pl.multiple_of(h * LANES + t * 8, 8), 8)
+            target = pl.ds(pl.multiple_of(t * 8, 8), 8)
             for c in range(C):
-                lo = c * LANES
-                values = [
-                    (recvy[j, rows, lo:lo + LANES], recvy[j, rows, A + lo:A + lo + LANES])
-                    for j in range(F)
-                ]
+                re_at, im_at = pl.ds(c * W, LANES), pl.ds(c * W + LANES, LANES)
+                values = [(recvy[j, rows, re_at], recvy[j, rows, im_at]) for j in range(F)]
                 for b, (re, im) in enumerate(block_dft(values, 1.0)):
-                    z[b, rows, lo:lo + LANES] = re
-                    z[b, rows, A + lo:A + lo + LANES] = im
+                    z[b, target, re_at] = re
+                    z[b, target, im_at] = im
 
         span = pl.ds(h * LANES, LANES)
 
         @pl.loop(0, F)
         def _(b):
-            re, im = halves(z[b, span, 0:A]), halves(z[b, span, A:2 * A])
-            line = exact_dot((t_ref[0, b], t_ref[1, b]), re, ((1,), (1,))) - exact_dot(
-                (t_ref[2, b], t_ref[3, b]), im, ((1,), (1,))
-            )
+            line = exact_dot((t_ref[0, b], t_ref[1, b]), halves(z[b]), ((1,), (1,)))
             gt[pl.ds(b, A, stride=F), :] = line * scale
 
         for j in range(N // LANES):
@@ -311,7 +317,7 @@
         out_specs=(vmem, vmem),
         scratch_shapes=[
             pltpu.VMEM((RC, N, LANES), f32),
-            pltpu.VMEM((F, R, 2 * A), f32),
+            pltpu.VMEM((F, LANES, 2 * A), f32),
             pltpu.VMEM((C, F, R, 2 * LANES), f32),
             pltpu.VMEM((C, F, R, 2 * LANES), f32),
             pltpu.VMEM((N, A), jnp.bfloat16),
@@ -324,8 +330,8 @@
             pltpu.VMEM((N, LANES), f32),
             pltpu.VMEM((R, N), f32),
             dma((2,)),
-            dma((C, F)), dma((C, F)),
-            dma((RC, F)), dma((RC, F)),
+            dma((C, RC, F)), dma((C, RC, F)),
+            dma((C, RC, F)), dma((C, RC, F)),
             dma((RC, CH)), dma((RC, CH)),
             dma((CH,)), dma((CH,)),
             dma((1 + RC,)),

time: 250 us -> 244 us (0.976); the launches traced: 245 us -> 242 us
  Pallas kernels: 212 us -> 209 us
    pallas_call x1, Pallas kernels: 212 us -> 209 us  [gradient_tiles(): pl.pallas_call(partial(kernel, F, CH), out_shape=(tile, tile), in_specs=[...]
  transfers between devices with their start and end apart: 4 -> 4, of which waited for: 1 -> 0; matrix products, arithmetic and copies ran while one was open for 2% -> 2% of each run, Pallas kernels for 86% -> 86%
where the time goes in v2:
time: 244 us; the launch traced here: 242 us
  Pallas kernels  209 us (86%)
  other arithmetic  14 us (6%)
  starting transfers between devices  10.2 us (4%)
  local copies, waits for them, and re-layouts  7.78 us (3%)
    pallas_call x1, Pallas kernels, gradient_tiles(): pl.pallas_call(partial(kernel, F, CH), out_shape=(tile, tile), in_specs=[...  209 us
    ppermute x4, starting transfers between devices, passed_along(): return lax.ppermute(x, axis, pairs)  10.2 us
    sub x1, other arithmetic, shards(): extrapolated = 2.0 * image_next - image_tile  6.55 us
  transfers between devices with their start and end apart: 4, of which 0 were waited for; matrix products, arithmetic and copies ran while one was open for 2% of the time, Pallas kernels for 86%

profile of v2, /device:TPU:9, one launch (start us, length us, event | category | flops | bytes accessed | tf_op | source)
XLA Modules:
  0.0 241.8 jit_solution(1332823099346152469)
XLA Ops:
  0.6 1.9 bitcast_convert_fusion.1
  2.5 0.0 copy-start.4
  2.5 0.0 copy-start.3
  2.5 1.3 copy-done.4
  3.8 3.8 %collective-permute-start = (f32[4,1,512]{2,1,0:T(1,128)S(1)}, f32[4,1,512]{2,1,0:T(1,128)S(1)}, u32[]{:S(2)}, u32[]{:S(2)}) collective-permute-start(f32[4,1,512]{2,1,0:T(1,128)S(1)} %slice.40), channel_id=1, source_target_pairs={{0,1},{1,2},{2,3},{3,4},{4,5},{5,6},{6,7},{8,9},{9,10},{10,11},{11... | collective-permute-start | bytes 24584 | tf_op jit(solution)/shard_map/ppermute | solution.py:21
  7.6 0.4 slice_reduce_fusion.1
  8.0 3.1 %collective-permute-start.1 = (f32[4,256]{1,0:T(4,128)S(1)}, f32[4,256]{1,0:T(4,128)S(1)}, u32[]{:S(2)}, u32[]{:S(2)}) collective-permute-start(f32[4,256]{1,0:T(4,128)S(1)} %slice_reduce_fusion.1), channel_id=1, source_target_pairs={{0,8},{8,16},{16,24},{1,9},{9,17},{17,25},{2,10},{10,18},{18,26},{... | collective-permute-start | bytes 12296 | tf_op jit(solution)/shard_map/ppermute | solution.py:21
  11.1 209.0 %shard_map.68 = (f32[4,256,512]{2,1,0:T(8,128)}, f32[4,256,512]{2,1,0:T(8,128)}) custom-call(f32[256,2048]{1,0:T(8,128)} %bitcast.39, bf16[2,8,256,512]{3,2,1,0:T(8,128)(2,1)} %constant.13.clone.t_ref, bf16[1,2048,256]{2,1,0:T(8,128)(2,1)} %w_hbm.1, bf16[1,2,2048,256]{3,2,1,0:T(8,128)(2,1)} %m_hbm.1), custom_call_target="tpu_custom_call" | custom-call | tf_op jit(solution)/shard_map/pallas_call | solution.py:313
  220.1 0.0 copy-done.3
  220.1 0.0 collective-permute-done.1
  220.2 0.2 copy.19
  220.4 0.0 collective-permute-done
  220.4 6.5 %multiply_subtract_fusion = (f32[4,256,512]{2,1,0:T(8,128)S(1)}, f32[4,256,512]{2,1,0:T(8,128)}) fusion(f32[4,256,512]{2,1,0:T(8,128)} %get-tuple-element.4, f32[4,256,512]{2,1,0:T(8,128)} %get-tuple-element.5, bf16[4,2,256,512]{3,2,1,0:T(8,128)(2,1)} %param.8, f32[4,256,511]{2,1,0:T(8,128)} %bitcast.37, f32[4,256,1]{2,1,0:T(8,128)S(1)} %copy.19, ...), kind=kLoop, calls=%fused_computation.16 | loop fusion | flops 6291456 | bytes 14680064 | tf_op jit(solution)/shard_map/sub | solution.py:357
  226.9 2.0 collective-permute-start.2
  229.0 0.2 slice_reduce_fusion
  229.2 1.3 collective-permute-start.3
  230.5 1.9 slice.46
  232.4 1.6 slice.44
  234.0 0.0 collective-permute-done.3
  234.0 0.2 copy.20
  234.3 0.0 collective-permute-done.2
  234.3 0.0 copy-start
  234.3 0.0 copy-start.1
  234.3 0.0 copy-start.2
  234.3 4.2 %add_reduce_fusion = f32[256,512]{1,0:T(8,128)S(1)} fusion(f32[4,256,512]{2,1,0:T(8,128)S(1)} %get-tuple-element.12, f32[4,1,512]{2,1,0:T(1,128)S(1)} %collective-permute-done.2, f32[4,255,512]{2,1,0:T(8,128)} %slice.44, bf16[4,2,256,512]{3,2,1,0:T(8,128)(2,1)} %param.8, f32[4,256,1]{2,1,0:T(8,128)S(1)} %copy.20, f32[4,256,511]{2,1,0:T(8,128)} %slice.46), kind=kLoop, calls=%fused_computation.15 | loop fusion | flops 7208960 | bytes 8912896 | tf_op jit(solution)/shard_map/reduce_sum | solution.py:366
  238.5 0.2 maximum_divide_fusion
  238.7 0.0 copy-done
  238.7 0.0 copy-done.1
  238.7 0.3 copy-done.2
  239.0 1.1 fusion.9
  240.1 0.2 pad_maximum_fusion
  240.3 1.5 copy.21
  (2 shorter events, 0.0 us)
Async XLA Ops:
  2.5 1.3 copy-start.4
  2.5 217.6 %copy-start.3 = (f32[4,256,512]{2,1,0:T(8,128)}, f32[4,256,512]{2,1,0:T(8,128)S(1)}, u32[]{:S(2)}) copy-start(f32[4,256,512]{2,1,0:T(8,128)S(1)} %get-tuple-element.17) | copy-start | bytes 6291460
  3.8 216.5 %collective-permute-start = (f32[4,1,512]{2,1,0:T(1,128)S(1)}, f32[4,1,512]{2,1,0:T(1,128)S(1)}, u32[]{:S(2)}, u32[]{:S(2)}) collective-permute-start(f32[4,1,512]{2,1,0:T(1,128)S(1)} %slice.40), channel_id=1, source_target_pairs={{0,1},{1,2},{2,3},{3,4},{4,5},{5,6},{6,7},{8,9},{9,10},{10,11},{11... | collective-permute-start | bytes 24584 | tf_op jit(solution)/shard_map/ppermute | solution.py:21
  8.0 212.2 %collective-permute-start.1 = (f32[4,256]{1,0:T(4,128)S(1)}, f32[4,256]{1,0:T(4,128)S(1)}, u32[]{:S(2)}, u32[]{:S(2)}) collective-permute-start(f32[4,256]{1,0:T(4,128)S(1)} %slice_reduce_fusion.1), channel_id=1, source_target_pairs={{0,8},{8,16},{16,24},{1,9},{9,17},{17,25},{2,10},{10,18},{18,26},{... | collective-permute-start | bytes 12296 | tf_op jit(solution)/shard_map/ppermute | solution.py:21
  226.9 7.3 %collective-permute-start.2 = (f32[4,1,512]{2,1,0:T(1,128)S(1)}, f32[4,1,512]{2,1,0:T(1,128)S(1)}, u32[]{:S(2)}, u32[]{:S(2)}) collective-permute-start(f32[4,1,512]{2,1,0:T(1,128)S(1)} %slice.45), channel_id=1, source_target_pairs={{1,0},{2,1},{3,2},{4,3},{5,4},{6,5},{7,6},{9,8},{10,9},{11,10},{12... | collective-permute-start | bytes 24584 | tf_op jit(solution)/shard_map/ppermute | solution.py:21
  229.2 4.8 %collective-permute-start.3 = (f32[4,256]{1,0:T(4,128)S(1)}, f32[4,256]{1,0:T(4,128)S(1)}, u32[]{:S(2)}, u32[]{:S(2)}) collective-permute-start(f32[4,256]{1,0:T(4,128)S(1)} %slice_reduce_fusion), channel_id=1, source_target_pairs={{8,0},{16,8},{24,16},{9,1},{17,9},{25,17},{10,2},{18,10},{26,18},{... | collective-permute-start | bytes 12296 | tf_op jit(solution)/shard_map/ppermute | solution.py:21
  234.3 4.4 %copy-start = (bf16[4,2,256,512]{3,2,1,0:T(8,128)(2,1)S(1)}, bf16[4,2,256,512]{3,2,1,0:T(8,128)(2,1)}, u32[]{:S(2)}) copy-start(bf16[4,2,256,512]{3,2,1,0:T(8,128)(2,1)} %param.8) | copy-start | bytes 6291460
  234.3 4.4 %copy-start.1 = (f32[4,256,511]{2,1,0:T(8,128)S(1)}, f32[4,256,511]{2,1,0:T(8,128)}, u32[]{:S(2)}) copy-start(f32[4,256,511]{2,1,0:T(8,128)} %slice.46) | copy-start | bytes 6279172
  234.3 4.7 %copy-start.2 = (f32[4,255,512]{2,1,0:T(8,128)S(1)}, f32[4,255,512]{2,1,0:T(8,128)}, u32[]{:S(2)}) copy-start(f32[4,255,512]{2,1,0:T(8,128)} %slice.44) | copy-start | bytes 6266884

commit v3 on v2

--- a/solution.py
+++ b/solution.py
@@ -13,12 +13,6 @@
 step_dual = 0.5
 clip_radius = 4.0
 LANES = 128
-
-
-def passed_along(x, axis, by):
-    devices = lax.axis_size(axis)
-    pairs = [(i, i + by) for i in range(devices) if 0 <= i + by < devices]
-    return lax.ppermute(x, axis, pairs)
 
 
 def turned(real, imag, num, den, sign):
@@ -90,10 +84,19 @@
     return found
 
 
+def halo_copy(source, target, send_sem, recv_sem, device):
+    return pltpu.make_async_remote_copy(
+        src_ref=source, dst_ref=target, send_sem=send_sem, recv_sem=recv_sem,
+        device_id=device, device_id_type=pl.DeviceIdType.MESH,
+    )
+
+
 def kernel(
-    F, CH, x_ref, t_ref, w_hbm, m_hbm, image_ref, grad_ref,
+    F, CH, x_ref, t_ref, w_hbm, m_hbm, d_hbm,
+    image_ref, grad_ref, up_ref, left_ref, low_ref, lowg_ref, right_ref, rightg_ref,
+    dual, up, left, low, right,
     xt, z, send, recv, wb, mb, wf, mf, u, sendy, recvy, gt, g,
-    in_sem, fs, fr, bs, br, cs, cr, xs, xr, ls,
+    in_sem, fs, fr, bs, br, cs, cr, xs, xr, ls, hs, hr, rs, rr, gs, gr,
 ):
     R, N = x_ref.shape
     A = N // F
@@ -110,6 +113,10 @@
     load_m = pltpu.make_async_copy(m_hbm.at[0], mb, in_sem.at[1])
     load_w.start()
     load_m.start()
+    load_d = pltpu.make_async_copy(d_hbm, dual, in_sem.at[2])
+    load_d.start()
+    above, below = lax.rem(me + F - 1, F), lax.rem(me + 1, F)
+    before, after = lax.rem(mine + CH - 1, CH), lax.rem(mine + 1, CH)
 
     barrier = pltpu.get_barrier_semaphore()
     for o in range(1, F):
@@ -122,7 +129,12 @@
             barrier, inc=1, device_id={"chan": lax.rem(mine + o, CH)},
             device_id_type=pl.DeviceIdType.MESH,
         )
-    pl.semaphore_wait(barrier, F - 1 + CH - 1)
+        for f in (above, below):
+            pl.semaphore_signal(
+                barrier, inc=1, device_id={"chan": lax.rem(mine + o, CH), "facet": f},
+                device_id_type=pl.DeviceIdType.MESH,
+            )
+    pl.semaphore_wait(barrier, F - 1 + 3 * (CH - 1))
 
     image_copies = []
     for o in range(1, CH):
@@ -183,6 +195,38 @@
             copy.start()
             group.append(copy)
         copies.append(group)
+
+    load_d.wait()
+    for k in range(CH):
+        up[k] = dual[k, 0, R - 16:R, :].astype(jnp.float32)[8:16, :]
+        left[k] = dual[k, 1, :, T - LANES:T].astype(jnp.float32)
+    halos = [
+        halo_copy(up, up_ref, hs.at[0], hr.at[0], {"facet": below}),
+        halo_copy(left, left_ref, hs.at[1], hr.at[1], {"chan": after}),
+    ]
+    for copy in halos:
+        copy.start()
+    for copy in image_copies + halos:
+        copy.wait()
+    for k in range(CH):
+        first_up = jnp.where(me > 0, up_ref[k], 0.0)[7:8, :]
+        first_left = jnp.where(mine > 0, left_ref[k], 0.0)[:, LANES - 1:LANES]
+        p = dual[k, 0, 0:16, :].astype(jnp.float32)[0:8, :]
+        q = dual[k, 1, 0:16, :].astype(jnp.float32)[0:8, :]
+        lane = lax.broadcasted_iota(jnp.int32, (8, T), 1)
+        q_prev = jnp.where(lane == 0, first_left[0:8, :], pltpu.roll(q, 1, 1))
+        low[k] = image_ref[k, 0:8, :] - (first_up - p + q_prev - q)
+        p = dual[k, 0, :, 0:LANES].astype(jnp.float32)
+        q = dual[k, 1, :, 0:LANES].astype(jnp.float32)
+        row = lax.broadcasted_iota(jnp.int32, (R, LANES), 0)
+        p_prev = jnp.where(row == 0, first_up[:, 0:LANES], pltpu.roll(p, 1, 0))
+        right[k] = image_ref[k, :, 0:LANES] - (p_prev - p + first_left - q)
+    edges = [
+        halo_copy(low, low_ref, hs.at[2], hr.at[2], {"facet": above}),
+        halo_copy(right, right_ref, hs.at[3], hr.at[3], {"chan": before}),
+    ]
+    for copy in edges:
+        copy.start()
 
     load_w.wait()
     load_m.wait()
@@ -279,8 +323,24 @@
 
         for j in range(N // LANES):
             g[span, j * LANES:(j + 1) * LANES] = gt[j * LANES:(j + 1) * LANES, :].T
+        if h == 0:
+            for o in range(CH):
+                d = lax.rem(mine + o, CH)
+                copy = halo_copy(
+                    g.at[0:8, pl.ds(pl.multiple_of(d * T, LANES), T)], lowg_ref.at[mine],
+                    gs.at[o], gr.at[o], {"chan": d, "facet": above},
+                )
+                copy.start()
+                last.append(copy)
         for o in range(1, CH):
             d = lax.rem(mine + o, CH)
+            e = lax.rem(mine + o + 1, CH)
+            copy = halo_copy(
+                g.at[span, pl.ds(pl.multiple_of(e * T, LANES), LANES)],
+                rightg_ref.at[mine, span], rs.at[h, o], rr.at[h, o], {"chan": d},
+            )
+            copy.start()
+            last.append(copy)
             copy = pltpu.make_async_remote_copy(
                 src_ref=g.at[span, pl.ds(pl.multiple_of(d * T, LANES), T)],
                 dst_ref=grad_ref.at[mine, span],
@@ -295,27 +355,41 @@
         )
         copy.start()
         last.append(copy)
-    for copy in image_copies + last:
+        copy = pltpu.make_async_copy(
+            g.at[span, pl.ds(pl.multiple_of(after * T, LANES), LANES)],
+            rightg_ref.at[mine, span], rr.at[h, 0],
+        )
+        copy.start()
+        last.append(copy)
+    for copy in edges + last:
         copy.wait()
 
 
-def gradient_tiles(F, CH, image, weights, measured):
+def gradient_tiles(F, CH, image, weights, measured, dual):
     R, N = image.shape
     A = N // F
     C = A // LANES
     RC = R // LANES
     table = jnp.asarray(tables(F, A))
-    tile = jax.ShapeDtypeStruct((CH, R, N // CH), jnp.float32)
+    T = N // CH
+    tile = jax.ShapeDtypeStruct((CH, R, T), jnp.float32)
+    line = jax.ShapeDtypeStruct((CH, 8, T), jnp.float32)
+    side = jax.ShapeDtypeStruct((CH, R, LANES), jnp.float32)
     f32 = jnp.float32
     dma = pltpu.SemaphoreType.DMA
     vmem = pl.BlockSpec(memory_space=pltpu.VMEM)
     hbm = pl.BlockSpec(memory_space=pl.ANY)
     return pl.pallas_call(
         partial(kernel, F, CH),
-        out_shape=(tile, tile),
-        in_specs=[vmem, vmem, hbm, hbm],
-        out_specs=(vmem, vmem),
+        out_shape=(tile, tile, line, side, line, line, side, side),
+        in_specs=[vmem, vmem, hbm, hbm, hbm],
+        out_specs=(vmem,) * 8,
         scratch_shapes=[
+            pltpu.VMEM((CH, 2, R, T), jnp.bfloat16),
+            pltpu.VMEM((CH, 8, T), f32),
+            pltpu.VMEM((CH, R, LANES), f32),
+            pltpu.VMEM((CH, 8, T), f32),
+            pltpu.VMEM((CH, R, LANES), f32),
             pltpu.VMEM((RC, N, LANES), f32),
             pltpu.VMEM((F, LANES, 2 * A), f32),
             pltpu.VMEM((C, F, R, 2 * LANES), f32),
@@ -329,44 +403,118 @@
             pltpu.VMEM((F, R, 2 * A), f32),
             pltpu.VMEM((N, LANES), f32),
             pltpu.VMEM((R, N), f32),
-            dma((2,)),
+            dma((3,)),
             dma((C, RC, F)), dma((C, RC, F)),
             dma((C, RC, F)), dma((C, RC, F)),
             dma((RC, CH)), dma((RC, CH)),
             dma((CH,)), dma((CH,)),
             dma((1 + RC,)),
+            dma((4,)), dma((4,)),
+            dma((RC, CH)), dma((RC, CH)),
+            dma((CH,)), dma((CH,)),
         ],
         compiler_params=pltpu.CompilerParams(
             collective_id=0, has_side_effects=True, vmem_limit_bytes=60 * 1024 * 1024
         ),
-    )(image, table, weights, measured)
+    )(image, table, weights, measured, dual)
+
+
+def prior_kernel(
+    n, edge, x, g, d, up, left, low, lowg, right, rightg, image, dual, ext, held, carry, parts
+):
+    t = pl.program_id(0)
+    CH, TR, T = x.shape
+    now = lax.rem(t, 2)
+    row = lax.broadcasted_iota(jnp.int32, (TR, T), 0)
+    lane = lax.broadcasted_iota(jnp.int32, (TR, T), 1)
+
+    @pl.when(t == 0)
+    def _():
+        carry[...] = jnp.where(edge[0] == 0, 0.0, up[...])
+
+    @pl.when(t < n)
+    def _():
+        for c in range(CH):
+            p = d[c, 0].astype(jnp.float32)
+            q = d[c, 1].astype(jnp.float32)
+            p_prev = jnp.where(row == 0, carry[c, 7:8, :], pltpu.roll(p, 1, 0))
+            first = jnp.where(edge[2] == 0, 0.0, left[c])[:, LANES - 1:LANES]
+            q_prev = jnp.where(lane == 0, first, pltpu.roll(q, 1, 1))
+            adjoint = p_prev - p + q_prev - q
+            value = x[c] - step_primal * (g[c] + adjoint)
+            image[c] = value
+            ext[now, c] = 2.0 * value - x[c]
+            held[now, c, 0] = p
+            held[now, c, 1] = q
+            carry[c] = p[TR - 8:TR, :]
+
+    @pl.when(t > 0)
+    def _():
+        was = 1 - now
+        total = jnp.zeros((TR, T), jnp.float32)
+        for c in range(CH):
+            e = ext[was, c]
+            beyond = jnp.where(edge[1] == 0, 0.0, low[c] - lowg[c])
+            following = jnp.where(t < n, ext[now, c, 0:8, :], beyond)[0:1, :]
+            rows = jnp.where(row == TR - 1, following, pltpu.roll(e, TR - 1, 0)) - e
+            side = jnp.where(edge[3] == 0, 0.0, right[c] - rightg[c])[:, 0:1]
+            cols = jnp.where(lane == T - 1, side, pltpu.roll(e, T - 1, 1)) - e
+            first_part = held[was, c, 0] + step_dual * rows
+            second_part = held[was, c, 1] + step_dual * cols
+            parts[c, 0] = first_part
+            parts[c, 1] = second_part
+            total = total + (first_part * first_part + second_part * second_part)
+        factor = 1.0 / jnp.maximum(1.0, jnp.sqrt(total) / clip_radius)
+        for c in range(CH):
+            dual[c, 0] = (parts[c, 0] * factor).astype(jnp.bfloat16)
+            dual[c, 1] = (parts[c, 1] * factor).astype(jnp.bfloat16)
+
+
+def prior(edge, x, g, dual, up, left, low, lowg, right, rightg):
+    CH, R, T = x.shape
+    TR = 32
+    n = R // TR
+    f32 = jnp.float32
+    ahead = lambda t: jnp.minimum(t, n - 1)
+    behind = lambda t: jnp.maximum(t - 1, 0)
+    tile = pl.BlockSpec((CH, TR, T), lambda t: (0, ahead(t), 0))
+    line = pl.BlockSpec((CH, 8, T), lambda t: (0, 0, 0))
+    return pl.pallas_call(
+        partial(prior_kernel, n),
+        grid=(n + 1,),
+        out_shape=(
+            jax.ShapeDtypeStruct((CH, R, T), f32),
+            jax.ShapeDtypeStruct((CH, 2, R, T), jnp.bfloat16),
+        ),
+        in_specs=[
+            pl.BlockSpec(memory_space=pltpu.SMEM),
+            tile,
+            tile,
+            pl.BlockSpec((CH, 2, TR, T), lambda t: (0, 0, ahead(t), 0)),
+            line,
+            pl.BlockSpec((CH, TR, LANES), lambda t: (0, ahead(t), 0)),
+            line,
+            line,
+            pl.BlockSpec((CH, TR, LANES), lambda t: (0, behind(t), 0)),
+            pl.BlockSpec((CH, TR, LANES), lambda t: (0, behind(t), 0)),
+        ],
+        out_specs=(tile, pl.BlockSpec((CH, 2, TR, T), lambda t: (0, 0, behind(t), 0))),
+        scratch_shapes=[
+            pltpu.VMEM((2, CH, TR, T), f32),
+            pltpu.VMEM((2, CH, 2, TR, T), f32),
+            pltpu.VMEM((CH, 8, T), f32),
+            pltpu.VMEM((CH, 2, TR, T), f32),
+        ],
+        compiler_params=pltpu.CompilerParams(vmem_limit_bytes=24 * 1024 * 1024),
+    )(edge, x, g, dual, up, left, low, lowg, right, rightg)
 
 
 def shards(image_field, weights, measured, dual_field):
-    image_tile, gradient_tile = gradient_tiles(
-        lax.axis_size("facet"), lax.axis_size("chan"), image_field[0], weights, measured
-    )
-    dual_rows = dual_field[:, 0].astype(jnp.float32)
-    dual_cols = dual_field[:, 1].astype(jnp.float32)
-    above = passed_along(dual_rows[:, -1:, :], "facet", 1)
-    leftward = passed_along(dual_cols[:, :, -1], "chan", 1)
-    prev_rows = jnp.concatenate([above, dual_rows[:, :-1, :]], axis=1)
-    prev_cols = jnp.concatenate([leftward[:, :, None], dual_cols[:, :, :-1]], axis=2)
-    adjoint = prev_rows - dual_rows + prev_cols - dual_cols
-    image_next = image_tile - step_primal * (gradient_tile + adjoint)
-    extrapolated = 2.0 * image_next - image_tile
-    below = passed_along(extrapolated[:, :1, :], "facet", -1)
-    rightward = passed_along(extrapolated[:, :, 0], "chan", -1)
-    diff_rows = jnp.concatenate([extrapolated[:, 1:, :], below], axis=1) - extrapolated
-    diff_cols = (
-        jnp.concatenate([extrapolated[:, :, 1:], rightward[:, :, None]], axis=2) - extrapolated
-    )
-    first_part = dual_rows + step_dual * diff_rows
-    second_part = dual_cols + step_dual * diff_cols
-    magnitude = jnp.sqrt(jnp.sum(first_part * first_part + second_part * second_part, axis=0))
-    factor = 1.0 / jnp.maximum(1.0, magnitude / clip_radius)
-    dual_next = jnp.stack([first_part * factor, second_part * factor], axis=1).astype(jnp.bfloat16)
-    return (image_next, dual_next)
+    F, CH = lax.axis_size("facet"), lax.axis_size("chan")
+    tiles = gradient_tiles(F, CH, image_field[0], weights, measured, dual_field)
+    f, c = lax.axis_index("facet"), lax.axis_index("chan")
+    edge = jnp.stack([f > 0, f < F - 1, c > 0, c < CH - 1]).astype(jnp.int32)
+    return prior(edge, tiles[0], tiles[1], dual_field, *tiles[2:])
 
 
 def solution(mesh):

time: 244 us -> 237 us (0.971)
  Pallas kernels: 209 us -> 226 us
  other arithmetic: 14 us -> 0.08 us
  starting transfers between devices: 10.2 us -> 0 us
    pallas_call x1 -> x2, Pallas kernels: 209 us -> 226 us  [the longest x1 219 us: gradient_tiles(): pl.pallas_call(partial(kernel, F, CH), out_shape=(tile, tile, line, side,...]
    ppermute x4 -> x0, starting transfers between devices: 10.2 us -> none  [passed_along(): return lax.ppermute(x, axis, pairs)]
    sub x1 -> x0, other arithmetic: 6.55 us -> none  [shards(): extrapolated = 2.0 * image_next - image_tile]
    unnamed x11 -> x18, local copies, waits for them, and re-layouts: 3.19 us -> 8.82 us
    reduce_sum x1 -> x0, other arithmetic: 4.15 us -> none  [shards(): jnp.sum(first_part * first_part + second_part * second_part, axis=0)]
    slice x6 -> x0, local copies, waits for them, and re-layouts: 4.15 us -> none  [the longest x1 1.94 us: shards(): extrapolated[:, :, 1:]]
  transfers between devices with their start and end apart: 4 -> 0, of which waited for: 0 -> 0; matrix products, arithmetic and copies ran while one was open for 2% -> 0% of each run, Pallas kernels for 86% -> 0%
where the time goes in v3:
time: 237 us; the launch traced here: 235 us
  Pallas kernels  226 us (95%)
  local copies, waits for them, and re-layouts  8.82 us (4%)
    pallas_call x1, Pallas kernels, gradient_tiles(): pl.pallas_call(partial(kernel, F, CH), out_shape=(tile, tile, line, side,...  219 us
    unnamed x18, local copies, waits for them, and re-layouts  8.82 us
    pallas_call x1, Pallas kernels, prior(): pl.pallas_call(partial(prior_kernel, n), grid=(n + 1,), out_shape=(jax.Sh...  6.46 us

profile of v3, /device:TPU:9, one launch (start us, length us, event | category | flops | bytes accessed | tf_op | source)
XLA Modules:
  0.0 235.4 jit_solution(8085916864719880106)
XLA Ops:
  0.6 0.1 add_convert_fusion.edge
  0.7 0.0 copy-start
  0.7 219.3 %shard_map.68 = (f32[4,256,512]{2,1,0:T(8,128)}, f32[4,256,512]{2,1,0:T(8,128)}, f32[4,8,512]{2,1,0:T(8,128)}, f32[4,256,128]{2,1,0:T(8,128)}, f32[4,8,512]{2,1,...) custom-call(f32[256,2048]{1,0:T(8,128)} %bitcast.5, ...), custom_call_target="tpu_custom_call" | custom-call | tf_op jit(solution)/shard_map/pallas_call | solution.py:382
  220.1 0.0 copy-done
  220.1 0.0 copy-start.1
  220.1 1.6 copy-done.1
  221.7 0.0 copy-start.2
  221.7 1.6 copy-done.2
  223.3 0.0 copy-start.3
  223.3 1.0 copy-done.3
  224.3 0.0 copy-start.4
  224.3 1.0 copy-done.4
  225.3 0.0 copy-start.5
  225.3 1.0 copy-done.5
  226.4 0.0 copy-start.6
  226.4 0.8 copy-done.6
  227.2 0.0 copy-start.7
  227.2 0.8 copy-done.7
  228.1 0.0 copy-start.8
  228.1 0.8 copy-done.8
  228.9 6.5 %shard_map.69 = (f32[4,256,512]{2,1,0:T(8,128)}, bf16[4,2,256,512]{3,2,1,0:T(8,128)(2,1)}) custom-call(s32[4]{0:T(128)S(1)} %add_convert_fusion.edge, f32[4,256,512]{2,1,0:T(8,128)S(1)} %copy-done.1, f32[4,256,512]{2,1,0:T(8,128)S(1)} %copy-done.2, bf16[4,2,256,512]{3,2,1,0:T(8,128)(2,1)S(1)} %copy-done, f32[4,8,512]{2,1,0:T(8,128)S(1)} %copy-done.6, ...), custom_call_target="tpu_custom_call" | custom-call | tf_op jit(solution)/shard_map/pallas_call | solution.py:482
Async XLA Ops:
  0.7 219.3 %copy-start = (bf16[4,2,256,512]{3,2,1,0:T(8,128)(2,1)S(1)}, bf16[4,2,256,512]{3,2,1,0:T(8,128)(2,1)}, u32[]{:S(2)}) copy-start(bf16[4,2,256,512]{3,2,1,0:T(8,128)(2,1)} %d.1) | copy-start | bytes 6291460
  220.1 1.6 copy-start.1
  221.7 1.6 copy-start.2
  223.3 1.0 copy-start.3
  224.3 1.0 copy-start.4
  225.3 1.0 copy-start.5
  226.4 0.8 copy-start.6
  227.2 0.8 copy-start.7
  228.1 0.8 copy-start.8

commit v4 on v3

--- a/solution.py
+++ b/solution.py
@@ -59,18 +59,48 @@
     return dot(fh, sh) + (dot(fh, sl) + dot(fl, sh))
 
 
-def tables(blocks, inner):
+def table_seeds(blocks, inner):
     n = blocks * inner
-    b = np.arange(blocks)[:, None, None]
-    a = np.arange(inner)[None, :, None]
-    i = np.arange(inner)[None, None, :]
-    phase = 2.0 * np.pi / n * (((blocks * a + b) * i) % n)
-    pair = np.stack([np.cos(phase), -np.sin(phase)], axis=2).astype(np.float32)
-    pair = pair.reshape(blocks, inner, 2, inner // LANES, LANES)
-    pair = pair.transpose(0, 1, 3, 2, 4).reshape(blocks, inner, 2 * inner)
-    high = pair.astype(jnp.bfloat16)
-    low = (pair - high.astype(np.float32)).astype(jnp.bfloat16)
-    return np.stack([high, low])
+    a = np.arange(max(blocks, inner))[:, None]
+    i = np.arange(inner)[None, :]
+
+    def pairs(step, count):
+        phase = 2.0 * np.pi / n * ((step * a[:count] * i) % n)
+        pair = np.stack([np.cos(phase), -np.sin(phase)], axis=1).astype(np.float32)
+        pair = pair.reshape(count, 2, inner // LANES, LANES)
+        return pair.transpose(0, 2, 1, 3).reshape(count, 2 * inner)
+
+    return pairs(blocks, inner), np.repeat(pairs(1, blocks)[:, None, :], 8, axis=1)
+
+
+def fill_tables(seed_ref, turn_ref, t_ref):
+    _, F, A, width = t_ref.shape
+
+    @pl.loop(0, F)
+    def _(b):
+        for c in range(width // (2 * LANES)):
+            re_at = slice(2 * c * LANES, (2 * c + 1) * LANES)
+            im_at = slice((2 * c + 1) * LANES, (2 * c + 2) * LANES)
+            turn_re, turn_im = turn_ref[b, 0:1, re_at], turn_ref[b, 0:1, im_at]
+
+            @pl.loop(0, A // 32)
+            def _(t):
+                rows = pl.ds(pl.multiple_of(t * 32, 32), 32)
+                re, im = seed_ref[rows, re_at], seed_ref[rows, im_at]
+                pair = (re * turn_re - im * turn_im, re * turn_im + im * turn_re)
+                for value, at in zip(pair, (re_at, im_at)):
+                    high, low = halves(value)
+                    t_ref[0, b, rows, at] = high
+                    t_ref[1, b, rows, at] = low
+
+
+def back_pieces(rows):
+    pieces, start = [], 0
+    while rows - start > 32:
+        size = min(LANES, (rows - start) // 2)
+        pieces.append((start, size))
+        start += size
+    return pieces + [(start, rows - start)]
 
 
 def square_tables(t_ref, k, chunks):
@@ -92,9 +122,9 @@
 
 
 def kernel(
-    F, CH, x_ref, t_ref, w_hbm, m_hbm, d_hbm,
-    image_ref, grad_ref, up_ref, left_ref, low_ref, lowg_ref, right_ref, rightg_ref,
-    dual, up, left, low, right,
+    F, CH, x_ref, seed_ref, turn_ref, w_hbm, m_hbm, d_hbm,
+    image_hbm, grad_ref, up_hbm, left_hbm, low_ref, lowg_ref, right_ref, rightg_ref,
+    t_ref, image_ref, up_ref, left_ref, dual, up, left, low, right,
     xt, z, send, recv, wb, mb, wf, mf, u, sendy, recvy, gt, g,
     in_sem, fs, fr, bs, br, cs, cr, xs, xr, ls, hs, hr, rs, rr, gs, gr,
 ):
@@ -134,6 +164,7 @@
                 barrier, inc=1, device_id={"chan": lax.rem(mine + o, CH), "facet": f},
                 device_id_type=pl.DeviceIdType.MESH,
             )
+    fill_tables(seed_ref, turn_ref, t_ref)
     pl.semaphore_wait(barrier, F - 1 + 3 * (CH - 1))
 
     image_copies = []
@@ -208,6 +239,11 @@
         copy.start()
     for copy in image_copies + halos:
         copy.wait()
+    edges = [
+        pltpu.make_async_copy(image_ref, image_hbm, in_sem.at[3]),
+        pltpu.make_async_copy(up_ref, up_hbm, in_sem.at[4]),
+        pltpu.make_async_copy(left_ref, left_hbm, in_sem.at[5]),
+    ]
     for k in range(CH):
         first_up = jnp.where(me > 0, up_ref[k], 0.0)[7:8, :]
         first_left = jnp.where(mine > 0, left_ref[k], 0.0)[:, LANES - 1:LANES]
@@ -221,7 +257,7 @@
         row = lax.broadcasted_iota(jnp.int32, (R, LANES), 0)
         p_prev = jnp.where(row == 0, first_up[:, 0:LANES], pltpu.roll(p, 1, 0))
         right[k] = image_ref[k, :, 0:LANES] - (p_prev - p + first_left - q)
-    edges = [
+    edges += [
         halo_copy(low, low_ref, hs.at[2], hr.at[2], {"facet": above}),
         halo_copy(right, right_ref, hs.at[3], hr.at[3], {"chan": before}),
     ]
@@ -240,7 +276,8 @@
             mf[c, 0, rows, :] = mb[0, rows, lo:lo + LANES].astype(jnp.float32)
             mf[c, 1, rows, :] = mb[1, rows, lo:lo + LANES].astype(jnp.float32)
 
-    back = [[] for _ in range(RC)]
+    pieces = back_pieces(R)
+    back = [[] for _ in pieces]
     for c in range(C):
         wide = slice(c * W, (c + 1) * W)
         for copy in copies[c]:
@@ -272,40 +309,40 @@
             u[k, :, 0:LANES] = p[:, 0:LANES] + q[:, LANES:]
             u[k, :, LANES:W] = p[:, LANES:] - q[:, 0:LANES]
 
-        for h in range(RC):
-
-            @pl.loop(0, LANES // 8)
+        for i, (start, size) in enumerate(pieces if c == C - 1 else [(0, R)]):
+
+            @pl.loop(0, size // 8)
             def _(t):
-                rows = pl.ds(pl.multiple_of(h * LANES + t * 8, 8), 8)
+                rows = pl.ds(pl.multiple_of(start + t * 8, 8), 8)
                 values = [(u[k, rows, 0:LANES], u[k, rows, LANES:W]) for k in range(F)]
                 for q, (re, im) in enumerate(block_dft(values, 1.0)):
                     sendy[q, rows, c * W:c * W + LANES] = re
                     sendy[q, rows, c * W + LANES:(c + 1) * W] = im
 
-            span = pl.ds(h * LANES, LANES)
+            span = pl.ds(start, size)
             for o in order:
                 d = lax.rem(me + o, F)
                 copy = pltpu.make_async_remote_copy(
                     src_ref=sendy.at[d, span, wide], dst_ref=recvy.at[me, span, wide],
-                    send_sem=bs.at[c, h, o], recv_sem=br.at[c, h, o],
+                    send_sem=bs.at[c, i, o], recv_sem=br.at[c, i, o],
                     device_id={"facet": d}, device_id_type=pl.DeviceIdType.MESH,
                 )
                 copy.start()
-                back[h].append(copy)
+                back[i].append(copy)
             copy = pltpu.make_async_copy(
-                sendy.at[me, span, wide], recvy.at[me, span, wide], br.at[c, h, 0]
+                sendy.at[me, span, wide], recvy.at[me, span, wide], br.at[c, i, 0]
             )
             copy.start()
-            back[h].append(copy)
+            back[i].append(copy)
 
     last = []
-    for h in range(RC):
+    for h, (start, size) in enumerate(pieces):
         for copy in back[h]:
             copy.wait()
 
-        @pl.loop(0, LANES // 8)
+        @pl.loop(0, size // 8)
         def _(t):
-            rows = pl.ds(pl.multiple_of(h * LANES + t * 8, 8), 8)
+            rows = pl.ds(pl.multiple_of(start + t * 8, 8), 8)
             target = pl.ds(pl.multiple_of(t * 8, 8), 8)
             for c in range(C):
                 re_at, im_at = pl.ds(c * W, LANES), pl.ds(c * W + LANES, LANES)
@@ -314,7 +351,7 @@
                     z[b, target, re_at] = re
                     z[b, target, im_at] = im
 
-        span = pl.ds(h * LANES, LANES)
+        span = pl.ds(start, size)
 
         @pl.loop(0, F)
         def _(b):
@@ -322,7 +359,7 @@
             gt[pl.ds(b, A, stride=F), :] = line * scale
 
         for j in range(N // LANES):
-            g[span, j * LANES:(j + 1) * LANES] = gt[j * LANES:(j + 1) * LANES, :].T
+            g[span, j * LANES:(j + 1) * LANES] = gt[j * LANES:(j + 1) * LANES, :].T[0:size, :]
         if h == 0:
             for o in range(CH):
                 d = lax.rem(mine + o, CH)
@@ -370,7 +407,8 @@
     A = N // F
     C = A // LANES
     RC = R // LANES
-    table = jnp.asarray(tables(F, A))
+    seed, turn = (jnp.asarray(t) for t in table_seeds(F, A))
+    PC = len(back_pieces(R))
     T = N // CH
     tile = jax.ShapeDtypeStruct((CH, R, T), jnp.float32)
     line = jax.ShapeDtypeStruct((CH, 8, T), jnp.float32)
@@ -382,9 +420,13 @@
     return pl.pallas_call(
         partial(kernel, F, CH),
         out_shape=(tile, tile, line, side, line, line, side, side),
-        in_specs=[vmem, vmem, hbm, hbm, hbm],
-        out_specs=(vmem,) * 8,
+        in_specs=[vmem, vmem, vmem, hbm, hbm, hbm],
+        out_specs=(hbm,) * 8,
         scratch_shapes=[
+            pltpu.VMEM((2, F, A, 2 * A), jnp.bfloat16),
+            pltpu.VMEM((CH, R, T), f32),
+            pltpu.VMEM((CH, 8, T), f32),
+            pltpu.VMEM((CH, R, LANES), f32),
             pltpu.VMEM((CH, 2, R, T), jnp.bfloat16),
             pltpu.VMEM((CH, 8, T), f32),
             pltpu.VMEM((CH, R, LANES), f32),
@@ -403,20 +445,20 @@
             pltpu.VMEM((F, R, 2 * A), f32),
             pltpu.VMEM((N, LANES), f32),
             pltpu.VMEM((R, N), f32),
-            dma((3,)),
+            dma((6,)),
             dma((C, RC, F)), dma((C, RC, F)),
-            dma((C, RC, F)), dma((C, RC, F)),
-            dma((RC, CH)), dma((RC, CH)),
+            dma((C, PC, F)), dma((C, PC, F)),
+            dma((PC, CH)), dma((PC, CH)),
             dma((CH,)), dma((CH,)),
-            dma((1 + RC,)),
+            dma((1 + PC,)),
             dma((4,)), dma((4,)),
-            dma((RC, CH)), dma((RC, CH)),
+            dma((PC, CH)), dma((PC, CH)),
             dma((CH,)), dma((CH,)),
         ],
         compiler_params=pltpu.CompilerParams(
             collective_id=0, has_side_effects=True, vmem_limit_bytes=60 * 1024 * 1024
         ),
-    )(image, table, weights, measured, dual)
+    )(image, seed, turn, weights, measured, dual)
 
 
 def prior_kernel(

time: 237 us -> 235 us (level)
  Pallas kernels: 226 us -> 223 us
    pallas_call x1, Pallas kernels: 219 us -> 216 us  [gradient_tiles(): pl.pallas_call(partial(kernel, F, CH), out_shape=(tile, tile, line, side,...]
where the time goes in v4:
time: 235 us; the launch traced here: 232 us
  Pallas kernels  223 us (95%)
  local copies, waits for them, and re-layouts  8.82 us (4%)
    pallas_call x1, Pallas kernels, gradient_tiles(): pl.pallas_call(partial(kernel, F, CH), out_shape=(tile, tile, line, side,...  216 us
    unnamed x18, local copies, waits for them, and re-layouts  8.82 us
    pallas_call x1, Pallas kernels, prior(): pl.pallas_call(partial(prior_kernel, n), grid=(n + 1,), out_shape=(jax.Sh...  6.46 us

profile of v4, /device:TPU:9, one launch (start us, length us, event | category | flops | bytes accessed | tf_op | source)
XLA Modules:
  0.0 232.3 jit_solution(2546081150251627669)
XLA Ops:
  0.6 0.1 add_convert_fusion.edge
  0.7 0.0 copy-start
  0.7 216.2 %shard_map.77 = (f32[4,256,512]{2,1,0:T(8,128)}, f32[4,256,512]{2,1,0:T(8,128)}, f32[4,8,512]{2,1,0:T(8,128)}, f32[4,256,128]{2,1,0:T(8,128)}, f32[4,8,512]{2,1,...) custom-call(f32[256,2048]{1,0:T(8,128)} %bitcast.5, ...), custom_call_target="tpu_custom_call" | custom-call | tf_op jit(solution)/shard_map/pallas_call | solution.py:420
  217.0 0.0 copy-done
  217.0 0.0 copy-start.1
  217.0 1.6 copy-done.1
  218.6 0.0 copy-start.2
  218.6 1.6 copy-done.2
  220.1 0.0 copy-start.3
  220.2 1.0 copy-done.3
  221.2 0.0 copy-start.4
  221.2 1.0 copy-done.4
  222.2 0.0 copy-start.5
  222.2 1.0 copy-done.5
  223.3 0.0 copy-start.6
  223.3 0.8 copy-done.6
  224.1 0.0 copy-start.7
  224.1 0.8 copy-done.7
  225.0 0.0 copy-start.8
  225.0 0.8 copy-done.8
  225.8 6.5 %shard_map.78 = (f32[4,256,512]{2,1,0:T(8,128)}, bf16[4,2,256,512]{3,2,1,0:T(8,128)(2,1)}) custom-call(s32[4]{0:T(128)S(1)} %add_convert_fusion.edge, f32[4,256,512]{2,1,0:T(8,128)S(1)} %copy-done.1, f32[4,256,512]{2,1,0:T(8,128)S(1)} %copy-done.2, bf16[4,2,256,512]{3,2,1,0:T(8,128)(2,1)S(1)} %copy-done, f32[4,8,512]{2,1,0:T(8,128)S(1)} %copy-done.6, ...), custom_call_target="tpu_custom_call" | custom-call | tf_op jit(solution)/shard_map/pallas_call | solution.py:524
Async XLA Ops:
  0.7 216.2 %copy-start = (bf16[4,2,256,512]{3,2,1,0:T(8,128)(2,1)S(1)}, bf16[4,2,256,512]{3,2,1,0:T(8,128)(2,1)}, u32[]{:S(2)}) copy-start(bf16[4,2,256,512]{3,2,1,0:T(8,128)(2,1)} %d.1) | copy-start | bytes 6291460
  217.0 1.6 copy-start.1
  218.6 1.6 copy-start.2
  220.1 1.0 copy-start.3
  221.2 1.0 copy-start.4
  222.2 1.0 copy-start.5
  223.3 0.8 copy-start.6
  224.1 0.8 copy-start.7
  225.0 0.8 copy-start.8

commit v5 on v4

--- a/solution.py
+++ b/solution.py
@@ -165,7 +165,18 @@
                 device_id_type=pl.DeviceIdType.MESH,
             )
     fill_tables(seed_ref, turn_ref, t_ref)
+    load_d.wait()
+    for k in range(CH):
+        up[k] = dual[k, 0, R - 16:R, :].astype(jnp.float32)[8:16, :]
+        left[k] = dual[k, 1, :, T - LANES:T].astype(jnp.float32)
     pl.semaphore_wait(barrier, F - 1 + 3 * (CH - 1))
+
+    halos = [
+        halo_copy(up, up_ref, hs.at[0], hr.at[0], {"facet": below}),
+        halo_copy(left, left_ref, hs.at[1], hr.at[1], {"chan": after}),
+    ]
+    for copy in halos:
+        copy.start()
 
     image_copies = []
     for o in range(1, CH):
@@ -226,43 +237,6 @@
             copy.start()
             group.append(copy)
         copies.append(group)
-
-    load_d.wait()
-    for k in range(CH):
-        up[k] = dual[k, 0, R - 16:R, :].astype(jnp.float32)[8:16, :]
-        left[k] = dual[k, 1, :, T - LANES:T].astype(jnp.float32)
-    halos = [
-        halo_copy(up, up_ref, hs.at[0], hr.at[0], {"facet": below}),
-        halo_copy(left, left_ref, hs.at[1], hr.at[1], {"chan": after}),
-    ]
-    for copy in halos:
-        copy.start()
-    for copy in image_copies + halos:
-        copy.wait()
-    edges = [
-        pltpu.make_async_copy(image_ref, image_hbm, in_sem.at[3]),
-        pltpu.make_async_copy(up_ref, up_hbm, in_sem.at[4]),
-        pltpu.make_async_copy(left_ref, left_hbm, in_sem.at[5]),
-    ]
-    for k in range(CH):
-        first_up = jnp.where(me > 0, up_ref[k], 0.0)[7:8, :]
-        first_left = jnp.where(mine > 0, left_ref[k], 0.0)[:, LANES - 1:LANES]
-        p = dual[k, 0, 0:16, :].astype(jnp.float32)[0:8, :]
-        q = dual[k, 1, 0:16, :].astype(jnp.float32)[0:8, :]
-        lane = lax.broadcasted_iota(jnp.int32, (8, T), 1)
-        q_prev = jnp.where(lane == 0, first_left[0:8, :], pltpu.roll(q, 1, 1))
-        low[k] = image_ref[k, 0:8, :] - (first_up - p + q_prev - q)
-        p = dual[k, 0, :, 0:LANES].astype(jnp.float32)
-        q = dual[k, 1, :, 0:LANES].astype(jnp.float32)
-        row = lax.broadcasted_iota(jnp.int32, (R, LANES), 0)
-        p_prev = jnp.where(row == 0, first_up[:, 0:LANES], pltpu.roll(p, 1, 0))
-        right[k] = image_ref[k, :, 0:LANES] - (p_prev - p + first_left - q)
-    edges += [
-        halo_copy(low, low_ref, hs.at[2], hr.at[2], {"facet": above}),
-        halo_copy(right, right_ref, hs.at[3], hr.at[3], {"chan": before}),
-    ]
-    for copy in edges:
-        copy.start()
 
     load_w.wait()
     load_m.wait()
@@ -334,6 +308,34 @@
             )
             copy.start()
             back[i].append(copy)
+
+        if c == 0:
+            for copy in image_copies + halos:
+                copy.wait()
+            edges = [
+                pltpu.make_async_copy(image_ref, image_hbm, in_sem.at[3]),
+                pltpu.make_async_copy(up_ref, up_hbm, in_sem.at[4]),
+                pltpu.make_async_copy(left_ref, left_hbm, in_sem.at[5]),
+            ]
+            for k in range(CH):
+                first_up = jnp.where(me > 0, up_ref[k], 0.0)[7:8, :]
+                first_left = jnp.where(mine > 0, left_ref[k], 0.0)[:, LANES - 1:LANES]
+                p = dual[k, 0, 0:16, :].astype(jnp.float32)[0:8, :]
+                q = dual[k, 1, 0:16, :].astype(jnp.float32)[0:8, :]
+                lane = lax.broadcasted_iota(jnp.int32, (8, T), 1)
+                q_prev = jnp.where(lane == 0, first_left[0:8, :], pltpu.roll(q, 1, 1))
+                low[k] = image_ref[k, 0:8, :] - (first_up - p + q_prev - q)
+                p = dual[k, 0, :, 0:LANES].astype(jnp.float32)
+                q = dual[k, 1, :, 0:LANES].astype(jnp.float32)
+                row = lax.broadcasted_iota(jnp.int32, (R, LANES), 0)
+                p_prev = jnp.where(row == 0, first_up[:, 0:LANES], pltpu.roll(p, 1, 0))
+                right[k] = image_ref[k, :, 0:LANES] - (p_prev - p + first_left - q)
+            edges += [
+                halo_copy(low, low_ref, hs.at[2], hr.at[2], {"facet": above}),
+                halo_copy(right, right_ref, hs.at[3], hr.at[3], {"chan": before}),
+            ]
+            for copy in edges:
+                copy.start()
 
     last = []
     for h, (start, size) in enumerate(pieces):
@@ -547,7 +549,7 @@
             pltpu.VMEM((CH, 8, T), f32),
             pltpu.VMEM((CH, 2, TR, T), f32),
         ],
-        compiler_params=pltpu.CompilerParams(vmem_limit_bytes=24 * 1024 * 1024),
+        compiler_params=pltpu.CompilerParams(vmem_limit_bytes=60 * 1024 * 1024),
     )(edge, x, g, dual, up, left, low, lowg, right, rightg)
 
 

time: 235 us -> 227 us (0.966)
  local copies, waits for them, and re-layouts: 8.82 us -> 0 us
    unnamed x18 -> x0, local copies, waits for them, and re-layouts: 8.82 us -> none
where the time goes in v5:
time: 227 us; the launch traced here: 226 us
  Pallas kernels  225 us (99%)
    pallas_call x1, Pallas kernels, gradient_tiles(): pl.pallas_call(partial(kernel, F, CH), out_shape=(tile, tile, line, side,...  216 us
    pallas_call x1, Pallas kernels, prior(): pl.pallas_call(partial(prior_kernel, n), grid=(n + 1,), out_shape=(jax.Sh...  8.8 us

profile of v5, /device:TPU:9, one launch (start us, length us, event | category | flops | bytes accessed | tf_op | source)
XLA Modules:
  0.0 226.1 jit_solution(6104813858924565004)
XLA Ops:
  0.6 0.6 add_convert_fusion.edge
  1.2 216.1 %shard_map.77 = (f32[4,256,512]{2,1,0:T(8,128)}, f32[4,256,512]{2,1,0:T(8,128)}, f32[4,8,512]{2,1,0:T(8,128)}, f32[4,256,128]{2,1,0:T(8,128)}, f32[4,8,512]{2,1,...) custom-call(f32[256,2048]{1,0:T(8,128)} %bitcast.5, ...), custom_call_target="tpu_custom_call" | custom-call | tf_op jit(solution)/shard_map/pallas_call | solution.py:422
  217.3 8.8 %shard_map.78 = (f32[4,256,512]{2,1,0:T(8,128)}, bf16[4,2,256,512]{3,2,1,0:T(8,128)(2,1)}) custom-call(s32[4]{0:T(128)} %add_convert_fusion.edge, f32[4,256,512]{2,1,0:T(8,128)} %get-tuple-element.10.x, f32[4,256,512]{2,1,0:T(8,128)} %get-tuple-element.11.g, bf16[4,2,256,512]{3,2,1,0:T(8,128)(2,1)} %d.1, f32[4,8,512]{2,1,0:T(8,128)} %get-tuple-element.12.up, ...), custom_call_target="tpu_custom_call" | custom-call | tf_op jit(solution)/shard_map/pallas_call | solution.py:526

commit v6 on v5

--- a/solution.py
+++ b/solution.py
@@ -516,7 +516,7 @@
 
 def prior(edge, x, g, dual, up, left, low, lowg, right, rightg):
     CH, R, T = x.shape
-    TR = 32
+    TR = 64
     n = R // TR
     f32 = jnp.float32
     ahead = lambda t: jnp.minimum(t, n - 1)

time: 227 us -> 225 us (level)
  no operation moved by 1% of the time
where the time goes in v6:
time: 225 us; the launch traced here: 224 us
  Pallas kernels  223 us (99%)
    pallas_call x1, Pallas kernels, gradient_tiles(): pl.pallas_call(partial(kernel, F, CH), out_shape=(tile, tile, line, side,...  216 us
    pallas_call x1, Pallas kernels, prior(): pl.pallas_call(partial(prior_kernel, n), grid=(n + 1,), out_shape=(jax.Sh...  7.02 us

profile of v6, /device:TPU:9, one launch (start us, length us, event | category | flops | bytes accessed | tf_op | source)
XLA Modules:
  0.0 224.4 jit_solution(1568974513401581892)
XLA Ops:
  0.6 0.6 add_convert_fusion.edge
  1.2 216.1 %shard_map.77 = (f32[4,256,512]{2,1,0:T(8,128)}, f32[4,256,512]{2,1,0:T(8,128)}, f32[4,8,512]{2,1,0:T(8,128)}, f32[4,256,128]{2,1,0:T(8,128)}, f32[4,8,512]{2,1,...) custom-call(f32[256,2048]{1,0:T(8,128)} %bitcast.5, ...), custom_call_target="tpu_custom_call" | custom-call | tf_op jit(solution)/shard_map/pallas_call | solution.py:422
  217.3 7.0 %shard_map.78 = (f32[4,256,512]{2,1,0:T(8,128)}, bf16[4,2,256,512]{3,2,1,0:T(8,128)(2,1)}) custom-call(s32[4]{0:T(128)} %add_convert_fusion.edge, f32[4,256,512]{2,1,0:T(8,128)} %get-tuple-element.10.x, f32[4,256,512]{2,1,0:T(8,128)} %get-tuple-element.11.g, bf16[4,2,256,512]{3,2,1,0:T(8,128)(2,1)} %d.1, f32[4,8,512]{2,1,0:T(8,128)} %get-tuple-element.12.up, ...), custom_call_target="tpu_custom_call" | custom-call | tf_op jit(solution)/shard_map/pallas_call | solution.py:526
